TPU v7x, 32 devices: a whole 2x2x4 slice. The times are simulated.
32 devices in a mesh: fsdp: 2 (over x), ctx: 4 (over y, core), tp: 4 (over z).
Axes of the slice: x: 2, y: 2, z: 4, core: 2. Of those that a mesh axis runs over, the one named last changes fastest.
Arguments:
- inputs: bfloat16 [8, 1024, 1024], P('fsdp', 'ctx'), may hold values from -6 to 6
- lengths: int32 [8], P('fsdp'), may hold values from 256 to 1024, as said below
- w_query: bfloat16 [1024, 1024], P(('fsdp', 'ctx'), 'tp'), may hold values from -0.1875 to 0.1875
- w_key: bfloat16 [1024, 1024], P(('fsdp', 'ctx'), 'tp'), may hold values from -0.1875 to 0.1875
- w_value: bfloat16 [1024, 1024], P(('fsdp', 'ctx'), 'tp'), may hold values from -0.1875 to 0.1875
- b_query: float32 [1024], P('tp'), may hold values from -3 to 3
- b_value: float32 [1024], P('tp'), may hold values from -3 to 3
- w_out: bfloat16 [1024, 1024], P(('fsdp', 'ctx'), 'tp'), may hold values from -2 to 2
- b_out: float32 [1024], replicated, may hold values from -3 to 3
- gain_attn: float32 [1024], replicated, may hold values from 0.5 to 1.5
- shift_attn: float32 [1024], replicated, may hold values from -3 to 3
- w_up: bfloat16 [1024, 4096], P(('fsdp', 'ctx'), 'tp'), may hold values from -0.1875 to 0.1875
- b_up: float32 [4096], P('tp'), may hold values from -3 to 3
- w_down: bfloat16 [1024, 4096], P(('fsdp', 'ctx'), 'tp'), may hold values from -0.125 to 0.125
- b_down: float32 [1024], replicated, may hold values from -3 to 3
- gain_ffn: float32 [1024], replicated, may hold values from 0.5 to 1.5
- shift_ffn: float32 [1024], replicated, may hold values from -3 to 3
- cotangent: bfloat16 [8, 1024, 1024], P('fsdp', 'ctx'), may hold values from -6 to 6
Outputs:
- result: bfloat16 [8, 1024, 1024], P('fsdp', 'ctx')
- grad_inputs: float32 [8, 1024, 1024], P('fsdp', 'ctx')
- grad_w_query: float32 [1024, 1024], P(('fsdp', 'ctx'), 'tp')
- grad_w_key: float32 [1024, 1024], P(('fsdp', 'ctx'), 'tp')
- grad_w_value: float32 [1024, 1024], P(('fsdp', 'ctx'), 'tp')
- grad_b_query: float32 [1024], P('tp')
- grad_b_value: float32 [1024], P('tp')
- grad_w_out: float32 [1024, 1024], P(('fsdp', 'ctx'), 'tp')
- grad_b_out: float32 [1024], replicated
- grad_gain_attn: float32 [1024], replicated
- grad_shift_attn: float32 [1024], replicated
- grad_w_up: float32 [1024, 4096], P(('fsdp', 'ctx'), 'tp')
- grad_b_up: float32 [4096], P('tp')
- grad_w_down: float32 [1024, 4096], P(('fsdp', 'ctx'), 'tp')
- grad_b_down: float32 [1024], replicated
- grad_gain_ffn: float32 [1024], replicated
- grad_shift_ffn: float32 [1024], replicated
Inputs may be any that keep to these rules, and one draw needn't show every extreme that they name: `lengths`: in each aligned group of 4 sequences one, drawn from the seed, has length 1024.
All inputs are finite; a program needn't handle non-finite values.
Results may differ from a plain program's by a relative error of at most 0.017.
Values may be sent and summed in bfloat16 or wider, within the bound.
A program may use at most 128 MiB of HBM per device.

v0:
```python
import math

import jax
import jax.numpy as jnp
from jax import lax
from jax.sharding import PartitionSpec as P

DH = 64


def layer_norm(hidden, gain, shift):
    row_mean = jnp.mean(hidden, -1, keepdims=True)
    centered = hidden - row_mean
    row_var = jnp.mean(centered * centered, -1, keepdims=True)
    return centered * lax.rsqrt(row_var + 1e-05) * gain + shift


def gelu_exact(pre_act):
    return jax.nn.gelu(pre_act, approximate=False)


def dot_last(left, right):
    return lax.dot_general(
        left, right, (((1,), (1,)), ((), ())), preferred_element_type=jnp.float32
    )


def dot_first(left, right):
    return lax.dot_general(
        left, right, (((0,), (0,)), ((), ())), preferred_element_type=jnp.float32
    )


def shards(
    inputs,
    lengths,
    w_query,
    w_key,
    w_value,
    b_query,
    b_value,
    w_out,
    b_out,
    gain_attn,
    shift_attn,
    w_up,
    b_up,
    w_down,
    b_down,
    gain_ffn,
    shift_ffn,
    cotangent,
):
    n_ctx = lax.axis_size("ctx")
    n_tensor = lax.axis_size("tp")
    seq_dev, seq_loc, width = inputs.shape
    seq_full = seq_loc * n_ctx
    head_dim = DH
    scale = 1.0 / math.sqrt(DH)
    tok_count = seq_dev * seq_loc
    flat_in = inputs.reshape(tok_count, width)
    first_pos = lax.axis_index("ctx") * seq_loc
    positions = first_pos + jnp.arange(seq_loc, dtype=jnp.int32)
    row_valid = positions[None, :] < lengths[:, None]
    key_valid = jnp.arange(seq_full, dtype=jnp.int32)[None, :] < lengths[:, None]
    grad_top = (cotangent.astype(jnp.float32) * row_valid[:, :, None].astype(jnp.float32)).reshape(
        tok_count, width
    )
    wq_all, wk_all, wv_all, wu_all, wo_all, wd_all = (
        lax.all_gather(w_query, ("fsdp", "ctx"), axis=0, tiled=True),
        lax.all_gather(w_key, ("fsdp", "ctx"), axis=0, tiled=True),
        lax.all_gather(w_value, ("fsdp", "ctx"), axis=0, tiled=True),
        lax.all_gather(w_up, ("fsdp", "ctx"), axis=0, tiled=True),
        lax.all_gather(w_out, ("fsdp", "ctx"), axis=0, tiled=True),
        lax.all_gather(w_down, ("fsdp", "ctx"), axis=0, tiled=True),
    )
    queries = (jnp.dot(flat_in, wq_all, preferred_element_type=jnp.float32) + b_query).astype(
        jnp.bfloat16
    )
    key_rows = jnp.dot(flat_in, wk_all, preferred_element_type=jnp.float32).astype(jnp.bfloat16)
    val_rows = (jnp.dot(flat_in, wv_all, preferred_element_type=jnp.float32) + b_value).astype(
        jnp.bfloat16
    )
    heads_tp = queries.shape[1] // head_dim

    def split_heads(matrix):
        return matrix.reshape(seq_dev, seq_loc, heads_tp, head_dim)

    qry_heads, key_heads, val_heads = (
        lax.all_to_all(split_heads(queries), "ctx", split_axis=2, concat_axis=1, tiled=True),
        lax.all_to_all(split_heads(key_rows), "ctx", split_axis=2, concat_axis=1, tiled=True),
        lax.all_to_all(split_heads(val_rows), "ctx", split_axis=2, concat_axis=1, tiled=True),
    )

    def scores_of(qry_seq, key_seq, key_ok):
        scores = (
            jnp.einsum("qhd,khd->hqk", qry_seq, key_seq, preferred_element_type=jnp.float32) * scale
        )
        return jnp.where(key_ok[None, None, :], scores, -1e30)

    def attend(packed):
        qry_seq, key_seq, val_seq, key_ok = packed
        scores = scores_of(qry_seq, key_seq, key_ok)
        row_top = jnp.max(scores, -1, keepdims=True)
        expo = jnp.exp(scores - row_top)
        row_total = jnp.sum(expo, -1, keepdims=True)
        attn_prob = expo / row_total
        log_total = (row_top + jnp.log(row_total))[..., 0]
        mixed = jnp.einsum(
            "hqk,khd->qhd",
            attn_prob.astype(jnp.bfloat16),
            val_seq,
            preferred_element_type=jnp.float32,
        )
        return (mixed.astype(jnp.bfloat16), log_total)

    attn_heads, log_totals = lax.map(attend, (qry_heads, key_heads, val_heads, key_valid))
    attn_tok = lax.all_to_all(attn_heads, "ctx", split_axis=1, concat_axis=2, tiled=True).reshape(
        tok_count, heads_tp * head_dim
    )
    share_rows = tok_count // n_tensor
    share_start = lax.axis_index("tp") * share_rows
    in_share = lax.dynamic_slice_in_dim(flat_in, share_start, share_rows, 0)
    attn_share = lax.psum_scatter(dot_last(attn_tok, wo_all), "tp", scatter_dimension=0, tiled=True)
    resid1 = in_share.astype(jnp.float32) + attn_share + b_out
    normed = layer_norm(resid1, gain_attn, shift_attn)
    normed_low = lax.all_gather(normed.astype(jnp.bfloat16), "tp", axis=0, tiled=True)
    pre_act = jnp.dot(normed_low, wu_all, preferred_element_type=jnp.float32) + b_up
    act_low = gelu_exact(pre_act).astype(jnp.bfloat16)
    down_share = lax.psum_scatter(dot_last(act_low, wd_all), "tp", scatter_dimension=0, tiled=True)
    resid2 = normed + down_share + b_down
    _, final_pull = jax.vjp(layer_norm, resid2, gain_ffn, shift_ffn)
    result_share = layer_norm(resid2, gain_ffn, shift_ffn).astype(jnp.bfloat16)
    top_share = lax.dynamic_slice_in_dim(grad_top, share_start, share_rows, 0)
    d_resid2, d_gain_ffn, d_shift_ffn = final_pull(top_share)
    d_bias_down = jnp.sum(d_resid2, 0)
    result_rows, d_resid2_low = (
        lax.all_gather(result_share, "tp", axis=0, tiled=True),
        lax.all_gather(d_resid2.astype(jnp.bfloat16), "tp", axis=0, tiled=True),
    )
    result = result_rows.reshape(inputs.shape)
    grad_wd = dot_first(d_resid2_low, act_low)
    d_act = jnp.dot(d_resid2_low, wd_all, preferred_element_type=jnp.float32)
    _, gelu_pull = jax.vjp(gelu_exact, pre_act)
    d_pre_low = gelu_pull(d_act)[0].astype(jnp.bfloat16)
    grad_wu = dot_first(normed_low, d_pre_low)
    d_bias_up = jnp.sum(d_pre_low.astype(jnp.float32), 0)
    d_normed = d_resid2 + lax.psum_scatter(
        dot_last(d_pre_low, wu_all), "tp", scatter_dimension=0, tiled=True
    )
    _, first_pull = jax.vjp(layer_norm, resid1, gain_attn, shift_attn)
    d_resid1_share, d_gain_attn, d_shift_attn = first_pull(d_normed)
    d_bias_out = jnp.sum(d_resid1_share, 0)
    partial_terms = jnp.stack(
        [d_bias_out, d_gain_attn, d_shift_attn, d_bias_down, d_gain_ffn, d_shift_ffn]
    )
    d_resid1, term_rows = (
        lax.all_gather(d_resid1_share.astype(jnp.bfloat16), "tp", axis=0, tiled=True).astype(
            d_resid1_share.dtype
        ),
        lax.all_gather(partial_terms.astype(jnp.bfloat16), "tp", axis=0, tiled=True).astype(
            partial_terms.dtype
        ),
    )
    summed_terms = jnp.sum(term_rows.reshape(n_tensor, 6, width), 0)
    d_bias_out = summed_terms[0]
    d_gain_attn = summed_terms[1]
    d_shift_attn = summed_terms[2]
    d_bias_down = summed_terms[3]
    d_gain_ffn = summed_terms[4]
    d_shift_ffn = summed_terms[5]
    d_resid1_low = d_resid1.astype(jnp.bfloat16)
    grad_wo = dot_first(d_resid1_low, attn_tok)
    d_attended = jnp.dot(d_resid1_low, wo_all, preferred_element_type=jnp.float32).astype(
        jnp.bfloat16
    )
    d_heads = lax.all_to_all(
        split_heads(d_attended), "ctx", split_axis=2, concat_axis=1, tiled=True
    )

    def attend_back(packed):
        qry_seq, key_seq, val_seq, key_ok, log_total, d_mixed = packed
        scores = scores_of(qry_seq, key_seq, key_ok)
        attn_prob = jnp.exp(scores - log_total[..., None])
        d_val = jnp.einsum(
            "hqk,qhd->khd",
            attn_prob.astype(jnp.bfloat16),
            d_mixed,
            preferred_element_type=jnp.float32,
        )
        d_prob = jnp.einsum("qhd,khd->hqk", d_mixed, val_seq, preferred_element_type=jnp.float32)
        row_delta = jnp.sum(attn_prob * d_prob, -1, keepdims=True)
        d_score = (attn_prob * (d_prob - row_delta)).astype(jnp.bfloat16)
        d_qry = (
            jnp.einsum("hqk,khd->qhd", d_score, key_seq, preferred_element_type=jnp.float32) * scale
        )
        d_key = (
            jnp.einsum("hqk,qhd->khd", d_score, qry_seq, preferred_element_type=jnp.float32) * scale
        )
        return (d_qry.astype(jnp.bfloat16), d_key.astype(jnp.bfloat16), d_val.astype(jnp.bfloat16))

    dq_heads, dk_heads, dv_heads = lax.map(
        attend_back, (qry_heads, key_heads, val_heads, key_valid, log_totals, d_heads)
    )
    dq_tok, dk_tok, dv_tok = (
        lax.all_to_all(dq_heads, "ctx", split_axis=1, concat_axis=2, tiled=True),
        lax.all_to_all(dk_heads, "ctx", split_axis=1, concat_axis=2, tiled=True),
        lax.all_to_all(dv_heads, "ctx", split_axis=1, concat_axis=2, tiled=True),
    )
    dq_tok = dq_tok.reshape(tok_count, heads_tp * head_dim)
    dk_tok = dk_tok.reshape(tok_count, heads_tp * head_dim)
    dv_tok = dv_tok.reshape(tok_count, heads_tp * head_dim)
    grad_wq = dot_first(flat_in, dq_tok)
    grad_wk = dot_first(flat_in, dk_tok)
    grad_wv = dot_first(flat_in, dv_tok)
    d_bias_query = jnp.sum(dq_tok.astype(jnp.float32), 0)
    d_bias_value = jnp.sum(dv_tok.astype(jnp.float32), 0)
    input_part = dot_last(dq_tok, wq_all) + dot_last(dk_tok, wk_all) + dot_last(dv_tok, wv_all)
    grad_inputs = (
        lax.psum(input_part.astype(jnp.bfloat16), "tp").astype(jnp.float32) + d_resid1
    ).reshape(inputs.shape)
    sum_wq, sum_wk, sum_wv, sum_wu, sum_wo, sum_wd = (
        lax.psum_scatter(grad_wq, ("fsdp", "ctx"), scatter_dimension=0, tiled=True),
        lax.psum_scatter(grad_wk, ("fsdp", "ctx"), scatter_dimension=0, tiled=True),
        lax.psum_scatter(grad_wv, ("fsdp", "ctx"), scatter_dimension=0, tiled=True),
        lax.psum_scatter(grad_wu, ("fsdp", "ctx"), scatter_dimension=0, tiled=True),
        lax.psum_scatter(grad_wo, ("fsdp", "ctx"), scatter_dimension=0, tiled=True),
        lax.psum_scatter(grad_wd, ("fsdp", "ctx"), scatter_dimension=0, tiled=True),
    )
    small_sums = lax.psum(
        (
            d_bias_query,
            d_bias_value,
            d_bias_up,
            d_bias_out,
            d_gain_attn,
            d_shift_attn,
            d_bias_down,
            d_gain_ffn,
            d_shift_ffn,
        ),
        ("fsdp", "ctx"),
    )
    sum_bq, sum_bv, sum_bu, sum_bo, sum_ga, sum_sa, sum_bd, sum_gf, sum_sf = small_sums
    return (
        result,
        grad_inputs,
        sum_wq,
        sum_wk,
        sum_wv,
        sum_bq,
        sum_bv,
        sum_wo,
        sum_bo,
        sum_ga,
        sum_sa,
        sum_wu,
        sum_bu,
        sum_wd,
        sum_bd,
        sum_gf,
        sum_sf,
    )


def solution(mesh):
    return jax.shard_map(
        shards,
        mesh=mesh,
        in_specs=(
            P("fsdp", "ctx", None),
            P("fsdp"),
            P(("fsdp", "ctx"), "tp"),
            P(("fsdp", "ctx"), "tp"),
            P(("fsdp", "ctx"), "tp"),
            P("tp"),
            P("tp"),
            P(("fsdp", "ctx"), "tp"),
            P(),
            P(),
            P(),
            P(("fsdp", "ctx"), "tp"),
            P("tp"),
            P(("fsdp", "ctx"), "tp"),
            P(),
            P(),
            P(),
            P("fsdp", "ctx", None),
        ),
        out_specs=(
            P("fsdp", "ctx", None),
            P("fsdp", "ctx", None),
            P(("fsdp", "ctx"), "tp"),
            P(("fsdp", "ctx"), "tp"),
            P(("fsdp", "ctx"), "tp"),
            P("tp"),
            P("tp"),
            P(("fsdp", "ctx"), "tp"),
            P(),
            P(),
            P(),
            P(("fsdp", "ctx"), "tp"),
            P("tp"),
            P(("fsdp", "ctx"), "tp"),
            P(),
            P(),
            P(),
        ),
        check_vma=False,
    )
```

profile of v0, /device:TPU:0, one launch (start us, length us, event | category | flops | bytes accessed | tf_op | source)
XLA Modules:
  0.0 932.9 jit_solution(6868604086081284882)
XLA Ops:
  8.0 11.6 %all_gather.33 = bf16[1024,256]{1,0:T(8,128)(2,1)S(1)} all-gather(bf16[128,256]{1,0:T(8,128)(2,1)} %param.26), channel_id=1, replica_groups=mesh['fsdp'=2,'ctx'=4,'tp'=4] {'fsdp','ctx'}, dimensions={0}, use_global_device_ids=true | all-gather | bytes 589824 | tf_op jit(solution)/shard_map/all_gather | solution.py:72
  24.3 3.5 all-to-all-start
  27.8 13.8 %all_gather.34 = bf16[1024,256]{1,0:T(8,128)(2,1)S(1)} all-gather(bf16[128,256]{1,0:T(8,128)(2,1)S(1)} %copy-done.22), channel_id=1, replica_groups=mesh['fsdp'=2,'ctx'=4,'tp'=4] {'fsdp','ctx'}, dimensions={0}, use_global_device_ids=true | all-gather | bytes 589824 | tf_op jit(solution)/shard_map/all_gather | solution.py:70
  46.3 3.5 all-to-all-start.1
  49.8 13.4 %all_gather.35 = bf16[1024,256]{1,0:T(8,128)(2,1)S(1)} all-gather(bf16[128,256]{1,0:T(8,128)(2,1)S(1)} %copy-done.23), channel_id=1, replica_groups=mesh['fsdp'=2,'ctx'=4,'tp'=4] {'fsdp','ctx'}, dimensions={0}, use_global_device_ids=true | all-gather | bytes 589824 | tf_op jit(solution)/shard_map/all_gather | solution.py:71
  69.8 4.4 all-to-all-start.2
  80.4 2.8 all-to-all-done.2
  87.7 18.3 %while.26 = (s32[]{:T(128)}, bf16[4,1024,1,64]{1,3,2,0:T(8,128)(2,1)}, f32[4,1,1024]{2,1,0:T(1,128)S(1)}, bf16[4,1024,1,64]{1,3,2,0:T(8,128)(2,1)}, pred[4,1024]...) while((s32[]{:T(128)}, ...), condition=%wide.region_3.4_spmd, body=%wide.region_0.3_spmd.sunk | while | flops 281082880 | bytes 13155421 | solution.py:117
  89.4 2.8 fusion.141
  94.0 2.8 fusion.141
  98.6 2.8 fusion.141
  103.2 2.8 fusion.141
  108.6 2.6 reshape.348
  111.1 4.1 all-to-all-start.3
  115.3 14.5 %all_gather.36 = bf16[1024,256]{1,0:T(8,128)(2,1)} all-gather(bf16[128,256]{1,0:T(8,128)(2,1)S(1)} %copy-done.24), channel_id=1, replica_groups=mesh['fsdp'=2,'ctx'=4,'tp'=4] {'fsdp','ctx'}, dimensions={0}, use_global_device_ids=true | all-gather | bytes 589824 | tf_op jit(solution)/shard_map/all_gather | solution.py:74
  132.4 2.5 copy.182
  137.3 3.8 fusion.76
  141.8 76.6 %reduce-scatter.10.cloned.1.call-done = f32[256,1024]{1,0:T(8,128)} async-done(((f32[1024,1024]{1,0:T(8,128)}), f32[256,1024]{1,0:T(8,128)}) %reduce-scatter.10.cloned.1.call-update) | async-done | bytes 1048592 | tf_op jit(solution)/shard_map/reduce_scatter | solution.py:124
  222.4 45.0 %all-gather.8.cloned.1.call-done = bf16[1024,1024]{1,0:T(8,128)(2,1)} async-done(((bf16[256,1024]{1,0:T(8,128)(2,1)}), bf16[1024,1024]{1,0:T(8,128)(2,1)}) %all-gather.8.cloned.1.call-update) | async-done | bytes 2097168 | tf_op jit(solution)/shard_map/all_gather | solution.py:127
  267.4 14.9 %multiply_convert_fusion.1 = (bf16[1024,1024]{1,0:T(8,128)(2,1)}, f32[1024,1024]{1,0:T(8,128)}, f32[1024,1024]{1,0:T(8,128)}) fusion(f32[1024]{0:T(1024)S(1)} %copy-done.33, bf16[1024,1024]{1,0:T(8,128)(2,1)} %all-gather.8.cloned.1.call-done, bf16[1024,1024]{1,0:T(8,128)(2,1)} %all-gather.10.cloned.1.call-done), kind=kOutput, calls=%fused_computation.72 | convolution fusion | flops 2216689664 | bytes 14684160 | tf_op jit(solution)/shard_map/dot_general | solution.py:128
  282.3 13.6 %all-gather.12.cloned.1.call-done = bf16[1024,1024]{1,0:T(8,128)(2,1)} async-done(((bf16[128,1024]{1,0:T(8,128)(2,1)}), bf16[1024,1024]{1,0:T(8,128)(2,1)}) %all-gather.12.cloned.1.call-update) | async-done | bytes 2097168 | tf_op jit(solution)/shard_map/all_gather | solution.py:75
  295.9 6.6 fusion.77
  302.6 4.0 convert_multiply_fusion
  306.5 72.8 %reduce-scatter.12.cloned.1.call-done = f32[256,1024]{1,0:T(8,128)} async-done(((f32[1024,1024]{1,0:T(8,128)}), f32[256,1024]{1,0:T(8,128)}) %reduce-scatter.12.cloned.1.call-update) | async-done | bytes 1048592 | tf_op jit(solution)/shard_map/reduce_scatter | solution.py:130
  385.9 46.0 %all-gather.16.cloned.1.call-done = bf16[1024,1024]{1,0:T(8,128)(2,1)} async-done(((bf16[256,1024]{1,0:T(8,128)(2,1)}), bf16[1024,1024]{1,0:T(8,128)(2,1)}) %all-gather.16.cloned.1.call-update) | async-done | bytes 2097168 | tf_op jit(solution)/shard_map/all_gather | solution.py:139
  431.8 8.4 convert_reduce_fusion
  441.6 4.4 fusion.78
  446.0 75.7 %reduce-scatter.14.cloned.1.call-done = f32[256,1024]{1,0:T(8,128)} async-done(((f32[1024,1024]{1,0:T(8,128)}), f32[256,1024]{1,0:T(8,128)}) %reduce-scatter.14.cloned.1.call-update) | async-done | bytes 1048592 | tf_op jit(solution)/shard_map/reduce_scatter | solution.py:148
  525.2 46.5 %all-gather.18.cloned.1.call-done = bf16[1024,1024]{1,0:T(8,128)(2,1)} async-done(((bf16[256,1024]{1,0:T(8,128)(2,1)}), bf16[1024,1024]{1,0:T(8,128)(2,1)}) %all-gather.18.cloned.1.call-update) | async-done | bytes 2097168 | tf_op jit(solution)/shard_map/all_gather | solution.py:158
  571.7 3.2 convolution_convert_fusion
  579.3 4.1 all-to-all-start.4
  584.2 8.1 all-to-all-done.4
  599.3 37.7 %while.27 = (s32[]{:T(128)}, bf16[4,1024,1,64]{1,3,2,0:T(8,128)(2,1)}, bf16[4,1024,1,64]{1,3,2,0:T(8,128)(2,1)}, bf16[4,1024,1,64]{1,3,2,0:T(8,128)(2,1)}, bf16[...) while((s32[]{:T(128)}, ...), condition=%wide.region_17.18_spmd, body=%wide.region_15.17_spmd.sunk | while | flops 687143936 | bytes 34904208 | solution.py:202
  640.2 12.3 %all_to_all.132 = bf16[4,2,32768]{2,1,0:T(2,128)(2,1)S(1)} all-to-all(bf16[4,2,32768]{2,1,0:T(2,128)(2,1)} %reshape.350), channel_id=1, replica_groups=mesh['fsdp'=2,'ctx'=4,'tp'=4] {'ctx'}, dimensions={0} | all-to-all | bytes 1048576 | tf_op jit(solution)/shard_map/all_to_all | solution.py:206
  662.0 11.9 %all_to_all.133 = bf16[4,2,32768]{2,1,0:T(2,128)(2,1)} all-to-all(bf16[4,2,32768]{2,1,0:T(2,128)(2,1)S(1)} %reshape.352), channel_id=1, replica_groups=mesh['fsdp'=2,'ctx'=4,'tp'=4] {'ctx'}, dimensions={0} | all-to-all | bytes 1048576 | tf_op jit(solution)/shard_map/all_to_all | solution.py:207
  683.0 2.6 reshape.354
  685.6 13.3 %all_to_all.134 = bf16[4,2,32768]{2,1,0:T(2,128)(2,1)} all-to-all(bf16[4,2,32768]{2,1,0:T(2,128)(2,1)} %reshape.354), channel_id=1, replica_groups=mesh['fsdp'=2,'ctx'=4,'tp'=4] {'ctx'}, dimensions={0} | all-to-all | bytes 1048576 | tf_op jit(solution)/shard_map/all_to_all | solution.py:208
  701.4 2.6 copy.185
  713.1 6.5 fusion.83
  721.2 6.0 fusion.82
  730.9 14.1 %all-gather = bf16[4,6,1024]{2,1,0:T(8,128)(2,1)S(1)} all-gather(bf16[1,6,1024]{2,1,0:T(8,128)(2,1)S(1)} %bitcast.278), channel_id=1, replica_groups=mesh['fsdp'=2,'ctx'=4,'tp'=4] {'tp'}, dimensions={0}, use_global_device_ids=true | all-gather | bytes 61440 | tf_op jit(solution)/shard_map/all_gather | solution.py:161
  747.0 24.0 %all-reduce = (f32[256]{0:T(256)}, f32[256]{0:T(256)}, f32[1024]{0:T(1024)}, f32[1024]{0:T(1024)}, f32[1024]{0:T(1024)}, /*index=5*/f32[1024]{0:T(1024)}, f32[1024]{0:T(1024)}, f32[1024]{0:T(1024)}, f32[1024]{0:T(1024)}) all-reduce(f32[256]{0:T(256)S(1)} %reduce_sum.198, ...), channel_id=1, replica_groups=mesh['fsdp'=2,'ctx'=4,'tp'=4] {'fsdp','ctx'}, use_global_device_ids=true, to_apply=%region_23.24 | all-reduce | flops 7680 | bytes 61440 | tf_op jit(solution)/shard_map/psum | solution.py:230
  776.0 22.9 %all-reduce.3.cloned.1.call-done = bf16[1024,1024]{1,0:T(8,128)(2,1)} async-done(((bf16[1024,1024]{1,0:T(8,128)(2,1)}), bf16[1024,1024]{1,0:T(8,128)(2,1)}) %all-reduce.3.cloned.1.call-update) | async-done | bytes 2097168 | tf_op jit(solution)/shard_map/psum | solution.py:220
  798.9 4.5 convert_add_fusion
  803.4 23.5 %reduce-scatter.26.cloned.1.call-done = f32[128,1024]{1,0:T(8,128)} async-done(((f32[1024,1024]{1,0:T(8,128)}), f32[128,1024]{1,0:T(8,128)}) %reduce-scatter.26.cloned.1.call-update) | async-done | bytes 524304 | tf_op jit(solution)/shard_map/reduce_scatter | solution.py:228
  826.9 55.5 %reduce-scatter.24.cloned.1.call-done = f32[128,1024]{1,0:T(8,128)} async-done(((f32[1024,1024]{1,0:T(8,128)}), f32[128,1024]{1,0:T(8,128)}) %reduce-scatter.24.cloned.1.call-update) | async-done | bytes 524304 | tf_op jit(solution)/shard_map/reduce_scatter | solution.py:226
  882.4 39.6 %reduce-scatter.22.cloned.1.call-done = f32[128,256]{1,0:T(8,128)} async-done(((f32[1024,256]{1,0:T(8,128)}), f32[128,256]{1,0:T(8,128)}) %reduce-scatter.22.cloned.1.call-update) | async-done | bytes 131088 | tf_op jit(solution)/shard_map/reduce_scatter | solution.py:227
  922.0 3.1 copy.220
  (261 shorter events, 152.0 us)
Async XLA Ops:
  20.4 7.3 copy-start.22
  20.4 21.9 %copy-start = (bf16[4,256,1024]{2,1,0:T(8,128)(2,1)S(1)}, bf16[4,256,1024]{2,1,0:T(8,128)(2,1)}, u32[]{:S(2)}) copy-start(bf16[4,256,1024]{2,1,0:T(8,128)(2,1)} %param.22) | copy-start | bytes 6291460
  20.4 21.9 %copy-start.34 = (f32[256]{0:T(256)S(1)}, f32[256]{0:T(256)}, u32[]{:S(2)}) copy-start(f32[256]{0:T(256)} %param.27) | copy-start | bytes 3076
  24.3 22.0 %all-to-all-start = ((bf16[4,256,4,64]{1,0,3,2:T(4,128)(2,1)}), bf16[4,256,4,64]{1,0,3,2:T(4,128)(2,1)S(1)}, u32[]{:S(2)}, u32[]{:S(2)}) async-start(bf16[4,256,4,64]{1,0,3,2:T(4,128)(2,1)} %reshape.321), calls=%async_computation | async-start | bytes 1048576 | tf_op jit(solution)/shard_map/all_to_all | solution.py:92
  42.4 7.4 copy-start.23
  46.3 23.6 %all-to-all-start.1 = ((bf16[4,256,4,64]{1,0,3,2:T(4,128)(2,1)}), bf16[4,256,4,64]{1,0,3,2:T(4,128)(2,1)S(1)}, u32[]{:S(2)}, u32[]{:S(2)}) async-start(bf16[4,256,4,64]{1,0,3,2:T(4,128)(2,1)} %reshape.322), calls=%async_computation.1 | async-start | bytes 1048576 | tf_op jit(solution)/shard_map/all_to_all | solution.py:90
  64.1 10.2 %copy-start.30 = (s32[4]{0:T(128)S(1)}, s32[4]{0:T(128)}, u32[]{:S(2)}) copy-start(s32[4]{0:T(128)} %param.23) | copy-start | bytes 52
  69.8 13.3 %all-to-all-start.2 = ((bf16[4,256,4,64]{1,0,3,2:T(4,128)(2,1)}), bf16[4,256,4,64]{1,0,3,2:T(4,128)(2,1)}, u32[]{:S(2)}, u32[]{:S(2)}) async-start(bf16[4,256,4,64]{1,0,3,2:T(4,128)(2,1)} %reshape.323), calls=%async_computation.2 | async-start | bytes 1048576 | tf_op jit(solution)/shard_map/all_to_all | solution.py:91
  106.0 30.4 %copy-start.2 = (bf16[4,1024,1,64]{1,3,2,0:T(8,128)(2,1)}, bf16[4,1024,1,64]{1,3,2,0:T(8,128)(2,1)S(1)}, u32[]{:S(2)}) copy-start(bf16[4,1024,1,64]{1,3,2,0:T(8,128)(2,1)S(1)} %get-tuple-element.601) | copy-start | bytes 1572868
  106.0 30.4 %copy-start.4 = (bf16[4,1024,1,64]{1,3,2,0:T(8,128)(2,1)}, bf16[4,1024,1,64]{1,3,2,0:T(8,128)(2,1)S(1)}, u32[]{:S(2)}) copy-start(bf16[4,1024,1,64]{1,3,2,0:T(8,128)(2,1)S(1)} %get-tuple-element.602) | copy-start | bytes 1572868
  106.0 9.3 copy-start.24
  111.1 18.7 %all-to-all-start.3 = ((bf16[4,2,32768]{2,1,0:T(2,128)(2,1)}), bf16[4,2,32768]{2,1,0:T(2,128)(2,1)}, u32[]{:S(2)}, u32[]{:S(2)}) async-start(bf16[4,2,32768]{2,1,0:T(2,128)(2,1)} %reshape.348), calls=%async_computation.3 | async-start | bytes 1048576 | tf_op jit(solution)/shard_map/all_to_all | solution.py:118
  115.3 103.1 %reduce-scatter.10.cloned.1.call-start = ((), (), s32[]{:S(2)}) async-start(), calls=%async_computation.17 | async-start | bytes 5242880 | tf_op jit(solution)/shard_map/reduce_scatter | solution.py:124
  137.3 81.1 %copy-start.27 = (f32[1024]{0:T(1024)S(1)}, f32[1024]{0:T(1024)}, u32[]{:S(2)}) copy-start(f32[1024]{0:T(1024)} %param.30) | copy-start | bytes 12292
  141.1 79.0 %copy-start.21 = (f32[1024]{0:T(1024)S(1)}, f32[1024]{0:T(1024)}, u32[]{:S(2)}) copy-start(f32[1024]{0:T(1024)} %param.31) | copy-start | bytes 12292
  141.1 79.0 %copy-start.25 = (f32[1024]{0:T(1024)S(1)}, f32[1024]{0:T(1024)}, u32[]{:S(2)}) copy-start(f32[1024]{0:T(1024)} %param.32) | copy-start | bytes 12292
  141.2 126.2 %copy-start.33 = (f32[1024]{0:T(1024)S(1)}, f32[1024]{0:T(1024)}, u32[]{:S(2)}) copy-start(f32[1024]{0:T(1024)} %param.34) | copy-start | bytes 12292
  141.2 81.2 %all-gather.10.cloned.1.call-start = ((), (), s32[]{:S(2)}) async-start(), calls=%async_computation.19 | async-start | bytes 2359296 | tf_op jit(solution)/shard_map/all_gather | solution.py:73
  141.7 125.6 %all-gather.8.cloned.1.call-start = ((), (), s32[]{:S(2)}) async-start(), calls=%async_computation.18 | async-start | bytes 2621440 | tf_op jit(solution)/shard_map/all_gather | solution.py:127
  221.2 74.7 %all-gather.12.cloned.1.call-start = ((), (), s32[]{:S(2)}) async-start(), calls=%async_computation.20 | async-start | bytes 2359296 | tf_op jit(solution)/shard_map/all_gather | solution.py:75
  221.8 157.6 %reduce-scatter.12.cloned.1.call-start = ((), (), s32[]{:S(2)}) async-start(), calls=%async_computation.21 | async-start | bytes 5242880 | tf_op jit(solution)/shard_map/reduce_scatter | solution.py:130
  302.4 76.9 %copy-start.28 = (f32[1024]{0:T(1024)S(1)}, f32[1024]{0:T(1024)}, u32[]{:S(2)}) copy-start(f32[1024]{0:T(1024)} %param.36) | copy-start | bytes 12292
  302.4 129.4 %all-gather.16.cloned.1.call-start = ((), (), s32[]{:S(2)}) async-start(), calls=%async_computation.23 | async-start | bytes 2621440 | tf_op jit(solution)/shard_map/all_gather | solution.py:139
  302.6 78.8 %copy-start.26 = (f32[1024]{0:T(1024)S(1)}, f32[1024]{0:T(1024)}, u32[]{:S(2)}) copy-start(f32[1024]{0:T(1024)} %param.37) | copy-start | bytes 12292
  306.5 75.8 %copy-start.29 = (f32[1024]{0:T(1024)S(1)}, f32[1024]{0:T(1024)}, u32[]{:S(2)}) copy-start(f32[1024]{0:T(1024)} %param.38) | copy-start | bytes 12292
  379.3 2.5 copy-start.7
  385.6 136.1 %reduce-scatter.14.cloned.1.call-start = ((), (), s32[]{:S(2)}) async-start(), calls=%async_computation.24 | async-start | bytes 5242880 | tf_op jit(solution)/shard_map/reduce_scatter | solution.py:148
  431.8 9.7 %copy-start.32 = (bf16[1024,1024]{1,0:T(8,128)(2,1)S(1)}, bf16[1024,1024]{1,0:T(8,128)(2,1)}, u32[]{:S(2)}) copy-start(bf16[1024,1024]{1,0:T(8,128)(2,1)} %all-gather.10.cloned.1.call-done) | copy-start | bytes 6291460
  446.0 125.7 %all-gather.18.cloned.1.call-start = ((), (), s32[]{:S(2)}) async-start(), calls=%async_computation.25 | async-start | bytes 2621440 | tf_op jit(solution)/shard_map/all_gather | solution.py:158
  574.9 24.5 %copy-start.3 = (bf16[4,1024,1,64]{1,3,2,0:T(8,128)(2,1)S(1)}, bf16[4,1024,1,64]{1,3,2,0:T(8,128)(2,1)}, u32[]{:S(2)}) copy-start(bf16[4,1024,1,64]{1,3,2,0:T(8,128)(2,1)} %copy-done.2) | copy-start | bytes 1572868
  574.9 24.5 %copy-start.5 = (bf16[4,1024,1,64]{1,3,2,0:T(8,128)(2,1)S(1)}, bf16[4,1024,1,64]{1,3,2,0:T(8,128)(2,1)}, u32[]{:S(2)}) copy-start(bf16[4,1024,1,64]{1,3,2,0:T(8,128)(2,1)} %copy-done.4) | copy-start | bytes 1572868
  579.3 13.1 %all-to-all-start.4 = ((bf16[4,256,4,64]{1,0,3,2:T(4,128)(2,1)}), bf16[4,256,4,64]{1,0,3,2:T(4,128)(2,1)}, u32[]{:S(2)}, u32[]{:S(2)}) async-start(bf16[4,256,4,64]{1,0,3,2:T(4,128)(2,1)} %reshape.327), calls=%async_computation.7 | async-start | bytes 1048576 | tf_op jit(solution)/shard_map/all_to_all | solution.py:177
  583.4 147.3 %all-gather.14.cloned.1.call-start = ((), (), s32[]{:S(2)}) async-start(), calls=%async_computation.22 | async-start | bytes 2621440 | tf_op jit(solution)/shard_map/all_gather | solution.py:138
  584.0 187.0 %reduce-scatter.16.cloned.1.call-start = ((), (), s32[]{:S(2)}) async-start(), calls=%async_computation.27 | async-start | bytes 1179648 | tf_op jit(solution)/shard_map/reduce_scatter | solution.py:223
  654.0 4.7 copy-start.20
  658.7 114.0 %reduce-scatter.18.cloned.1.call-start = ((), (), s32[]{:S(2)}) async-start(), calls=%async_computation.28 | async-start | bytes 1179648 | tf_op jit(solution)/shard_map/reduce_scatter | solution.py:224
  680.7 93.7 %reduce-scatter.20.cloned.1.call-start = ((), (), s32[]{:S(2)}) async-start(), calls=%async_computation.29 | async-start | bytes 1179648 | tf_op jit(solution)/shard_map/reduce_scatter | solution.py:225
  708.1 2.0 copy-start.18
  708.1 2.8 copy-start.11
  708.1 2.8 copy-start.16
  708.1 90.8 %all-reduce.3.cloned.1.call-start = ((), (), s32[]{:S(2)}) async-start(), calls=%async_computation.26 | async-start | bytes 4194304 | tf_op jit(solution)/shard_map/psum | solution.py:220
  713.0 113.9 %reduce-scatter.26.cloned.1.call-start = ((), (), s32[]{:S(2)}) async-start(), calls=%async_computation.32 | async-start | bytes 4718592 | tf_op jit(solution)/shard_map/reduce_scatter | solution.py:228
  719.6 1.6 copy-start.31
  719.6 162.8 %reduce-scatter.24.cloned.1.call-start = ((), (), s32[]{:S(2)}) async-start(), calls=%async_computation.31 | async-start | bytes 4718592 | tf_op jit(solution)/shard_map/reduce_scatter | solution.py:226
  727.2 1.7 copy-start.1
  727.2 1.8 copy-start.9
  727.2 17.8 %copy-start.13 = (bf16[4,4,256,1,64]{2,1,4,0,3:T(4,128)(2,1)S(1)}, bf16[4,4,256,1,64]{2,1,4,0,3:T(4,128)(2,1)}, u32[]{:S(2)}) copy-start(bf16[4,4,256,1,64]{2,1,4,0,3:T(4,128)(2,1)} %copy-done.12) | copy-start | bytes 1572868
  727.2 194.8 %reduce-scatter.22.cloned.1.call-start = ((), (), s32[]{:S(2)}) async-start(), calls=%async_computation.30 | async-start | bytes 1179648 | tf_op jit(solution)/shard_map/reduce_scatter | solution.py:227
  (12 other events, 11.4 us)
Sparse Core Ops, SparseCore 0:
  141.3 77.0 reduce-scatter.9
  302.6 76.7 reduce-scatter.11
  525.3 46.3 all-gather.17
  585.6 45.1 all-gather.13
  713.1 85.7 all-reduce.2
Sparse Core Ops, SparseCore 1:
  143.7 28.0 all-gather.9
  221.3 46.0 all-gather.7
  269.3 26.5 all-gather.11
  385.7 46.0 all-gather.15
  446.1 75.6 reduce-scatter.13
  658.7 33.8 reduce-scatter.15
  695.6 37.0 reduce-scatter.17
  735.8 36.1 reduce-scatter.19
  775.7 51.1 reduce-scatter.25
  831.2 51.2 reduce-scatter.23
  886.1 35.9 reduce-scatter.21
where the time goes:
time: 940 us; the launch traced here: 933 us
  waiting for transfers between devices  530 us (56%)
  blocking collectives  129 us (14%)
  matrix products  116 us (12%)
  local copies, waits for them, and re-layouts  88.8 us (9%)
  other arithmetic  31.1 us (3%)
  starting transfers between devices  21.3 us (2%)
  between operations  16.6 us (2%)
    reduce_scatter x1, waiting for transfers between devices, shards(): lax.psum_scatter(dot_last(attn_tok, wo_all), 'tp', scatter_dimension=0, t...  76.6 us
    reduce_scatter x1, waiting for transfers between devices, shards(): lax.psum_scatter(dot_last(d_pre_low, wu_all), 'tp', scatter_dimension=0,...  75.7 us
    reduce_scatter x1, waiting for transfers between devices, shards(): lax.psum_scatter(dot_last(act_low, wd_all), 'tp', scatter_dimension=0, ti...  72.8 us
    reduce_scatter x1, waiting for transfers between devices, shards(): lax.psum_scatter(grad_wu, ('fsdp', 'ctx'), scatter_dimension=0, tiled=True)  55.5 us
    all_gather x1, waiting for transfers between devices, shards(): lax.all_gather(d_resid1_share.astype(jnp.bfloat16), 'tp', axis=0, tiled=T...  46.5 us
    all_gather x1, waiting for transfers between devices, shards(): lax.all_gather(d_resid2.astype(jnp.bfloat16), 'tp', axis=0, tiled=True)  46 us
    all_gather x1, waiting for transfers between devices, shards(): lax.all_gather(normed.astype(jnp.bfloat16), 'tp', axis=0, tiled=True)  45 us
    reduce_scatter x1, waiting for transfers between devices, shards(): lax.psum_scatter(grad_wo, ('fsdp', 'ctx'), scatter_dimension=0, tiled=True)  39.6 us
  transfers between devices with their start and end apart: 21, of which 13 were waited for; matrix products, arithmetic and copies ran while one was open for 15% of the time, Pallas kernels for 0%

commit v1 on v0

v1 whole, which is shorter than its diff:
```python
import math

import jax
import jax.numpy as jnp
from jax import lax
from jax.sharding import PartitionSpec as P

DH = 64


def layer_norm(hidden, gain, shift):
    row_mean = jnp.mean(hidden, -1, keepdims=True)
    centered = hidden - row_mean
    row_var = jnp.mean(centered * centered, -1, keepdims=True)
    return centered * lax.rsqrt(row_var + 1e-05) * gain + shift


def gelu_exact(pre_act):
    return jax.nn.gelu(pre_act, approximate=False)


def dot(left, right):
    return jnp.dot(left, right, preferred_element_type=jnp.float32)


def dot_last(left, right):
    return lax.dot_general(
        left, right, (((1,), (1,)), ((), ())), preferred_element_type=jnp.float32
    )


def dot_first(left, right):
    return lax.dot_general(
        left, right, (((0,), (0,)), ((), ())), preferred_element_type=jnp.float32
    )


def low(v):
    return v.astype(jnp.bfloat16)


def shards(
    inputs,
    lengths,
    w_query,
    w_key,
    w_value,
    b_query,
    b_value,
    w_out,
    b_out,
    gain_attn,
    shift_attn,
    w_up,
    b_up,
    w_down,
    b_down,
    gain_ffn,
    shift_ffn,
    cotangent,
):
    n_fsdp = lax.axis_size("fsdp")
    n_ctx = lax.axis_size("ctx")
    n_tp = lax.axis_size("tp")
    assert n_ctx == n_tp and inputs.shape[0] % n_tp == 0
    seq_dev, seq_loc, width = inputs.shape
    per_tp = seq_dev // n_tp
    seq_full = seq_loc * n_ctx
    scale = 1.0 / math.sqrt(DH)
    c_idx = lax.axis_index("ctx")
    t_idx = lax.axis_index("tp")
    swap = [(c * n_tp + t, t * n_tp + c) for c in range(n_ctx) for t in range(n_tp)]

    def gather_cols(block):
        moved = lax.ppermute(block, ("ctx", "tp"), swap)
        return lax.all_gather(moved, ("fsdp", "tp"), axis=0, tiled=True)

    def scatter_cols(grad):
        mine = lax.psum_scatter(low(grad), ("fsdp", "tp"), scatter_dimension=0, tiled=True)
        return lax.ppermute(mine, ("ctx", "tp"), swap).astype(jnp.float32)

    hid = w_query.shape[1]
    hid_ff = w_up.shape[1]
    attn_w = gather_cols(jnp.concatenate([w_query, w_key, w_value, w_out], axis=1))
    wqkv = attn_w[:, : 3 * hid]
    wo = attn_w[:, 3 * hid :]
    ffn_w = gather_cols(jnp.concatenate([w_up, w_down], axis=1))
    wu = ffn_w[:, :hid_ff]
    wd = ffn_w[:, hid_ff:]
    biases = lax.ppermute(jnp.concatenate([b_query, b_value, b_up]), ("ctx", "tp"), swap)
    bq = biases[:hid]
    bv = biases[hid : 2 * hid]
    bu = biases[2 * hid :]

    def to_tok(rows):
        return lax.all_gather(
            rows.reshape(per_tp, seq_loc, -1), "ctx", axis=1, tiled=True
        ).reshape(per_tp * seq_full, -1)

    def to_share(rows):
        return (
            lax.psum_scatter(
                low(rows).reshape(per_tp, seq_full, -1), "ctx", scatter_dimension=1, tiled=True
            )
            .reshape(per_tp * seq_loc, -1)
            .astype(jnp.float32)
        )

    first_seq = t_idx * per_tp
    in_share = lax.dynamic_slice_in_dim(inputs, first_seq, per_tp, 0).reshape(-1, width)
    ct_share = lax.dynamic_slice_in_dim(cotangent, first_seq, per_tp, 0).reshape(-1, width)
    len_share = lax.dynamic_slice_in_dim(lengths, first_seq, per_tp, 0)
    x_tok = to_tok(in_share)
    positions = c_idx * seq_loc + jnp.arange(seq_loc, dtype=jnp.int32)
    row_valid = (positions[None, :] < len_share[:, None]).reshape(-1, 1)
    key_valid = jnp.arange(seq_full, dtype=jnp.int32)[None, :] < len_share[:, None]

    qkv = dot(x_tok, wqkv)
    queries = low(qkv[:, :hid] + bq)
    keys = low(qkv[:, hid : 2 * hid])
    vals = low(qkv[:, 2 * hid :] + bv)
    heads = hid // DH

    def split(m):
        return m.reshape(per_tp, seq_full, heads, DH).transpose(0, 2, 1, 3)

    def join(m):
        return m.transpose(0, 2, 1, 3).reshape(per_tp * seq_full, heads * DH)

    qh, kh, vh = split(queries), split(keys), split(vals)
    scores = jnp.einsum("bhqd,bhkd->bhqk", qh, kh, preferred_element_type=jnp.float32) * scale
    scores = jnp.where(key_valid[:, None, None, :], scores, -1e30)
    row_top = jnp.max(scores, -1, keepdims=True)
    expo = jnp.exp(scores - row_top)
    row_total = jnp.sum(expo, -1, keepdims=True)
    prob = expo / row_total
    prob_low = low(prob)
    attended = join(low(jnp.einsum("bhqk,bhkd->bhqd", prob_low, vh, preferred_element_type=jnp.float32)))

    resid1 = in_share.astype(jnp.float32) + to_share(dot_last(attended, wo)) + b_out
    normed = layer_norm(resid1, gain_attn, shift_attn)
    normed_low = to_tok(low(normed))
    pre_act = dot(normed_low, wu) + bu
    act_low = low(gelu_exact(pre_act))
    resid2 = normed + to_share(dot_last(act_low, wd)) + b_down
    out_share, final_pull = jax.vjp(layer_norm, resid2, gain_ffn, shift_ffn)
    result = lax.all_gather(
        low(out_share).reshape(per_tp, seq_loc, width), "tp", axis=0, tiled=True
    )
    top_share = ct_share.astype(jnp.float32) * row_valid.astype(jnp.float32)
    d_resid2, d_gain_ffn, d_shift_ffn = final_pull(top_share)
    d_resid2_low = to_tok(low(d_resid2))
    grad_wd = dot_first(d_resid2_low, act_low)
    d_act = dot(d_resid2_low, wd)
    _, gelu_pull = jax.vjp(gelu_exact, pre_act)
    d_pre_low = low(gelu_pull(d_act)[0])
    grad_wu = dot_first(normed_low, d_pre_low)
    g_ffn = scatter_cols(jnp.concatenate([grad_wu, grad_wd], axis=1))
    d_normed = d_resid2 + to_share(dot_last(d_pre_low, wu))
    _, first_pull = jax.vjp(layer_norm, resid1, gain_attn, shift_attn)
    d_resid1, d_gain_attn, d_shift_attn = first_pull(d_normed)
    d_resid1_low = to_tok(low(d_resid1))
    grad_wo = dot_first(d_resid1_low, attended)
    d_att = split(low(dot(d_resid1_low, wo)))
    d_vals = jnp.einsum("bhqk,bhqd->bhkd", prob_low, d_att, preferred_element_type=jnp.float32)
    d_prob = jnp.einsum("bhqd,bhkd->bhqk", d_att, vh, preferred_element_type=jnp.float32)
    row_delta = jnp.sum(prob * d_prob, -1, keepdims=True)
    d_score = low(prob * (d_prob - row_delta))
    d_q = jnp.einsum("bhqk,bhkd->bhqd", d_score, kh, preferred_element_type=jnp.float32) * scale
    d_k = jnp.einsum("bhqk,bhqd->bhkd", d_score, qh, preferred_element_type=jnp.float32) * scale
    d_qkv = jnp.concatenate([join(low(d_q)), join(low(d_k)), join(low(d_vals))], axis=1)
    grad_qkv = dot_first(x_tok, d_qkv)
    g_attn = scatter_cols(jnp.concatenate([grad_qkv, grad_wo], axis=1))
    gi_share = d_resid1 + to_share(dot_last(d_qkv, wqkv))
    grad_inputs = lax.all_gather(
        low(gi_share).reshape(per_tp, seq_loc, width), "tp", axis=0, tiled=True
    ).astype(jnp.float32)

    col_sums = jnp.concatenate(
        [
            jnp.sum(d_qkv[:, :hid].astype(jnp.float32), 0),
            jnp.sum(d_qkv[:, 2 * hid :].astype(jnp.float32), 0),
            jnp.sum(d_pre_low.astype(jnp.float32), 0),
        ]
    )
    blocks = lax.dynamic_update_slice(
        jnp.zeros((n_ctx, col_sums.shape[0]), jnp.float32), col_sums[None], (c_idx, 0)
    )
    whole = jnp.stack(
        [
            jnp.sum(d_resid1, 0),
            d_gain_attn,
            d_shift_attn,
            jnp.sum(d_resid2, 0),
            d_gain_ffn,
            d_shift_ffn,
        ]
    )
    flat = lax.psum(jnp.concatenate([blocks.reshape(-1), whole.reshape(-1)]), ("fsdp", "ctx", "tp"))
    n_block = col_sums.shape[0]
    mine = lax.dynamic_slice_in_dim(flat, t_idx * n_block, n_block, 0)
    whole = flat[n_ctx * n_block :].reshape(6, width)
    return (
        result,
        grad_inputs,
        g_attn[:, :hid],
        g_attn[:, hid : 2 * hid],
        g_attn[:, 2 * hid : 3 * hid],
        mine[:hid],
        mine[hid : 2 * hid],
        g_attn[:, 3 * hid :],
        whole[0],
        whole[1],
        whole[2],
        g_ffn[:, :hid_ff],
        mine[2 * hid :],
        g_ffn[:, hid_ff:],
        whole[3],
        whole[4],
        whole[5],
    )


def solution(mesh):
    weight = P(("fsdp", "ctx"), "tp")
    acts = P("fsdp", "ctx", None)
    return jax.shard_map(
        shards,
        mesh=mesh,
        in_specs=(
            acts,
            P("fsdp"),
            weight,
            weight,
            weight,
            P("tp"),
            P("tp"),
            weight,
            P(),
            P(),
            P(),
            weight,
            P("tp"),
            weight,
            P(),
            P(),
            P(),
            acts,
        ),
        out_specs=(
            acts,
            acts,
            weight,
            weight,
            weight,
            P("tp"),
            P("tp"),
            weight,
            P(),
            P(),
            P(),
            weight,
            P("tp"),
            weight,
            P(),
            P(),
            P(),
        ),
        check_vma=False,
    )
```

time: 940 us -> 770 us (0.82)
  blocking collectives: 129 us -> 65.3 us
  local copies, waits for them, and re-layouts: 88.8 us -> 28.8 us
  waiting for transfers between devices: 530 us -> 508 us
  matrix products: 116 us -> 96.9 us
  starting transfers between devices: 21.3 us -> 5.07 us
  other arithmetic: 31.1 us -> 43 us
    reduce_scatter x9 -> x4, waiting for transfers between devices: 344 us -> 98.7 us  [to_share(): lax.psum_scatter(low(rows).reshape(per_tp, seq_full, -1), 'ctx', scatter_...]
    all_gather x6 -> x8, waiting for transfers between devices: 151 us -> 305 us  [the longest x2 127 us: gather_cols(): return lax.all_gather(moved, ('fsdp', 'tp'), axis=0, tiled=True)]
    unnamed x16, waiting for transfers between devices: 1.78 us -> 104 us
    all_gather x5 -> x0, blocking collectives: 67.5 us -> none  [the longest x1 14.5 us: shards(): lax.all_gather(w_out, ('fsdp', 'ctx'), axis=0, tiled=True)]
    psum x1, blocking collectives: 24 us -> 65.3 us  [shards(): lax.psum(jnp.concatenate([blocks.reshape(-1), whole.reshape(-1)]), ('fsdp...]
    all_to_all x3 -> x0, blocking collectives: 37.5 us -> none  [the longest x1 13.3 us: shards(): lax.all_to_all(dv_heads, 'ctx', split_axis=1, concat_axis=2, tiled=True)]
    all_to_all x16 -> x0, local copies, waits for them, and re-layouts: 26.9 us -> none  [the longest x2 4.45 us: shards(): lax.all_to_all(split_heads(d_attended), 'ctx', split_axis=2, concat_axis=...]
    psum x1 -> x0, waiting for transfers between devices: 22.9 us -> none  [shards(): lax.psum(input_part.astype(jnp.bfloat16), 'tp').astype(jnp.float32)]
  transfers between devices with their start and end apart: 21 -> 19, of which waited for: 13 -> 14; matrix products, arithmetic and copies ran while one was open for 15% -> 6% of each run, Pallas kernels for 0% -> 0%
where the time goes in v1:
time: 770 us; the launch traced here: 762 us
  waiting for transfers between devices  508 us (66%)
  matrix products  96.9 us (13%)
  blocking collectives  65.3 us (8%)
  other arithmetic  43 us (6%)
  local copies, waits for them, and re-layouts  28.8 us (4%)
  between operations  14.7 us (2%)
    all_gather x2, waiting for transfers between devices, gather_cols(): return lax.all_gather(moved, ('fsdp', 'tp'), axis=0, tiled=True)  127 us
    unnamed x16, waiting for transfers between devices  104 us
    reduce_scatter x4, waiting for transfers between devices, to_share(): lax.psum_scatter(low(rows).reshape(per_tp, seq_full, -1), 'ctx', scatter_...  98.7 us
    all_gather x4, waiting for transfers between devices, to_tok(): lax.all_gather(rows.reshape(per_tp, seq_loc, -1), 'ctx', axis=1, tiled=True)  89.2 us
    psum x1, blocking collectives, shards(): lax.psum(jnp.concatenate([blocks.reshape(-1), whole.reshape(-1)]), ('fsdp...  65.3 us
    all_gather x1, waiting for transfers between devices, shards(): lax.all_gather(low(out_share).reshape(per_tp, seq_loc, width), 'tp', axis...  45.8 us
    all_gather x1, waiting for transfers between devices, shards(): lax.all_gather(low(gi_share).reshape(per_tp, seq_loc, width), 'tp', axis=...  43.8 us
    dot_general x4, matrix products, dot(): return jnp.dot(left, right, preferred_element_type=jnp.float32)  29.8 us
  transfers between devices with their start and end apart: 19, of which 14 were waited for; matrix products, arithmetic and copies ran while one was open for 6% of the time, Pallas kernels for 0%

profile of v1, /device:TPU:0, one launch (start us, length us, event | category | flops | bytes accessed | tf_op | source)
XLA Modules:
  0.0 762.1 jit_solution(7233370961068989959)
XLA Ops:
  7.2 1.9 constant_dynamic-slice_fusion
  14.9 21.5 %all-gather.9.cloned.1.call-done = bf16[1,1024,1024]{2,1,0:T(8,128)(2,1)} async-done(((bf16[1,256,1024]{2,1,0:T(8,128)(2,1)}), bf16[1,1024,1024]{2,1,0:T(8,128)(2,1)}) %all-gather.9.cloned.1.call-update) | async-done | bytes 2097168 | tf_op jit(solution)/shard_map/all_gather | solution.py:96
  36.5 54.6 %all-gather.11.cloned.1.call-done = bf16[1024,1024]{1,0:T(8,128)(2,1)} async-done(((bf16[128,1024]{1,0:T(8,128)(2,1)}), bf16[1024,1024]{1,0:T(8,128)(2,1)}) %all-gather.11.cloned.1.call-update) | async-done | bytes 2097168 | tf_op jit(solution)/shard_map/all_gather | solution.py:76
  91.1 3.9 fusion.31
  95.3 9.5 %fusion.111 = (f32[4,1024]{1,0:T(4,128)S(1)}, f32[4,1024,1024]{1,2,0:T(8,128)}) fusion(pred[1024]{0:T(1024)(128)(4,1)S(1)} %iota_compare_fusion, bf16[4,1024,64]{1,2,0:T(8,128)(2,1)S(1)} %bitcast.174, bf16[4,1024,64]{1,2,0:T(8,128)(2,1)S(1)} %bitcast.172), kind=kOutput, calls=%fused_computation.159 | convolution fusion | flops 553649152 | bytes 17843200 | tf_op jit(solution)/shard_map/sub | solution.py:134
  104.7 7.3 fusion.50
  112.9 3.4 convert_bitcast_fusion.3
  118.0 31.5 %reduce-scatter.11.cloned.1.call-done = bf16[1,256,1024]{2,1,0:T(8,128)(2,1)} async-done(((bf16[1,1024,1024]{2,1,0:T(8,128)(2,1)}), bf16[1,256,1024]{2,1,0:T(8,128)(2,1)}) %reduce-scatter.11.cloned.1.call-update) | async-done | bytes 524304 | tf_op jit(solution)/shard_map/reduce_scatter | solution.py:102
  150.8 1.4 multiply_reduce_fusion.4
  152.2 2.2 fusion.87
  154.6 72.0 %all-gather.15.cloned.1.call-done = bf16[1024,2048]{1,0:T(8,128)(2,1)} async-done(((bf16[128,2048]{1,0:T(8,128)(2,1)}), bf16[1024,2048]{1,0:T(8,128)(2,1)}) %all-gather.15.cloned.1.call-update) | async-done | bytes 4194320 | tf_op jit(solution)/shard_map/all_gather | solution.py:76
  226.6 23.0 %all-gather.13.cloned.1.call-done = bf16[1,1024,1024]{2,1,0:T(8,128)(2,1)} async-done(((bf16[1,256,1024]{2,1,0:T(8,128)(2,1)}), bf16[1,1024,1024]{2,1,0:T(8,128)(2,1)}) %all-gather.13.cloned.1.call-update) | async-done | bytes 2097168 | tf_op jit(solution)/shard_map/all_gather | solution.py:96
  249.6 15.0 %multiply_convert_fusion.1 = (bf16[1024,1024]{1,0:T(8,128)(2,1)S(1)}, f32[1024,1024]{1,0:T(8,128)}, f32[1024,1024]{1,0:T(8,128)}) fusion(f32[1024]{0:T(1024)S(1)} %slice.122, bf16[1024,2048]{1,0:T(8,128)(2,1)} %all-gather.15.cloned.1.call-done, bf16[1,1024,1024]{2,1,0:T(8,128)(2,1)} %all-gather.13.cloned.1.call-done), kind=kOutput, calls=%fused_computation.15 | convolution fusion | flops 2216689664 | bytes 14684160 | tf_op jit(solution)/shard_map/dot_general | solution.py:23
  265.9 3.7 convert_bitcast_fusion.2
  270.4 30.8 %reduce-scatter.13.cloned.1.call-done = bf16[1,256,1024]{2,1,0:T(8,128)(2,1)} async-done(((bf16[1,1024,1024]{2,1,0:T(8,128)(2,1)}), bf16[1,256,1024]{2,1,0:T(8,128)(2,1)}) %reduce-scatter.13.cloned.1.call-update) | async-done | bytes 524304 | tf_op jit(solution)/shard_map/reduce_scatter | solution.py:102
  301.2 1.8 fusion.103
  303.2 1.6 fusion.77
  306.2 2.3 fusion.100
  308.8 22.5 %all-gather.19.cloned.1.call-done = bf16[1,1024,1024]{2,1,0:T(8,128)(2,1)} async-done(((bf16[1,256,1024]{2,1,0:T(8,128)(2,1)}), bf16[1,1024,1024]{2,1,0:T(8,128)(2,1)}) %all-gather.19.cloned.1.call-update) | async-done | bytes 2097168 | tf_op jit(solution)/shard_map/all_gather | solution.py:96
  331.2 8.4 %convert_reduce_fusion = (f32[1024]{0:T(1024)S(1)}, bf16[1024,1024]{1,0:T(8,128)(2,1)S(1)}) fusion(f32[1024,1024]{1,0:T(8,128)} %get-tuple-element.69, bf16[1024,2048]{1,0:T(8,128)(2,1)} %all-gather.15.cloned.1.call-done, bf16[1,1024,1024]{2,1,0:T(8,128)(2,1)} %all-gather.19.cloned.1.call-done, f32[1024,1024]{1,0:T(8,128)} %get-tuple-element.92, ...), kind=kOutput, calls=%fused_computation.13 | convolution fusion | flops 2165308416 | bytes 14688256 | tf_op jit(solution)/shard_map/dot_general | solution.py:23
  341.0 3.7 convert_bitcast_fusion.1
  344.8 31.5 %reduce-scatter.15.cloned.1.call-done = bf16[1,256,1024]{2,1,0:T(8,128)(2,1)} async-done(((bf16[1,1024,1024]{2,1,0:T(8,128)(2,1)}), bf16[1,256,1024]{2,1,0:T(8,128)(2,1)}) %reduce-scatter.15.cloned.1.call-update) | async-done | bytes 524304 | tf_op jit(solution)/shard_map/reduce_scatter | solution.py:102
  376.3 2.2 multiply_reduce_fusion.1
  378.5 3.0 fusion.99
  381.5 1.6 fusion.97
  383.7 22.2 %all-gather.21.cloned.1.call-done = bf16[1,1024,1024]{2,1,0:T(8,128)(2,1)} async-done(((bf16[1,256,1024]{2,1,0:T(8,128)(2,1)}), bf16[1,1024,1024]{2,1,0:T(8,128)(2,1)}) %all-gather.21.cloned.1.call-update) | async-done | bytes 2097168 | tf_op jit(solution)/shard_map/all_gather | solution.py:96
  405.9 2.4 fusion.56
  408.4 8.6 %convert_reduce_fusion.1 = (f32[4,64]{1,0:T(4,128)S(1)}, bf16[4,1024,64]{1,2,0:T(8,128)(2,1)S(1)}) fusion(bf16[4,1024,64]{1,2,0:T(8,128)(2,1)S(1)} %bitcast.192, f32[4,1024,1024]{1,2,0:T(8,128)} %get-tuple-element.91, f32[4,1024]{1,0:T(4,128)S(1)} %get-tuple-element.90), kind=kOutput, calls=%fused_computation.110 | convolution fusion | flops 546045696 | bytes 17843200 | tf_op jit(solution)/shard_map/bhqk,bhqd->bhkd/dot_general | solution.py:165
  416.9 10.7 %multiply_reduce_fusion = (f32[4,1024]{1,0:T(4,128)S(1)}, f32[4,1024,1024]{1,2,0:T(8,128)}) fusion(f32[4,1024,1024]{1,2,0:T(8,128)} %get-tuple-element.91, f32[4,1024]{1,0:T(4,128)S(1)} %get-tuple-element.90, bf16[4,1024,64]{1,2,0:T(8,128)(2,1)S(1)} %bitcast.193, bf16[4,1024,64]{1,2,0:T(8,128)(2,1)S(1)} %bitcast.183), kind=kOutput, calls=%fused_computation.2 | convolution fusion | flops 549449728 | bytes 34635776 | tf_op jit(solution)/shard_map/bhqd,bhkd->bhqk/dot_general | solution.py:166
  427.6 11.8 %multiply_convert_fusion = bf16[4,1024,1024]{1,2,0:T(8,128)(2,1)S(1)} fusion(f32[4,1024,1024]{1,2,0:T(8,128)} %get-tuple-element.94, f32[4,1024]{1,0:T(4,128)S(1)} %get-tuple-element.93, f32[4,1024,1024]{1,2,0:T(8,128)} %get-tuple-element.91, f32[4,1024]{1,0:T(4,128)S(1)} %get-tuple-element.90), kind=kLoop, calls=%fused_computation.1 | loop fusion | flops 16777216 | bytes 41975808 | tf_op jit(solution)/shard_map/convert_element_type | solution.py:39
  439.4 2.7 fusion.62
  442.1 1.7 convert_reduce_fusion.2
  443.8 3.2 convert_bitcast_fusion
  448.0 4.8 fusion.38
  452.8 2.4 fusion.35
  455.2 2.5 pad_maximum_fusion
  457.7 6.5 copy.61
  465.3 2.3 fusion.59
  467.6 3.4 fusion.45
  471.1 2.6 copy.59
  473.8 4.8 reduce-scatter.17.cloned.1.call-done
  478.6 2.3 add_convert_fusion.1
  480.9 45.8 %all-gather.17.cloned.1.call-done = bf16[4,256,1024]{2,1,0:T(8,128)(2,1)} async-done(((bf16[1,256,1024]{2,1,0:T(8,128)(2,1)}), bf16[4,256,1024]{2,1,0:T(8,128)(2,1)}) %all-gather.17.cloned.1.call-update) | async-done | bytes 2097168 | tf_op jit(solution)/shard_map/all_gather | solution.py:147
  527.2 89.6 %reduce-scatter.21.cloned.1.call-done = bf16[128,2048]{1,0:T(8,128)(2,1)} async-done(((bf16[1024,2048]{1,0:T(8,128)(2,1)}), bf16[128,2048]{1,0:T(8,128)(2,1)}) %reduce-scatter.21.cloned.1.call-update) | async-done | bytes 524304
  618.9 65.3 %psum.7 = f32[12288]{0:T(1024)S(1)} all-reduce(f32[12288]{0:T(1024)S(1)} %pad_maximum_fusion.7), channel_id=1, replica_groups=mesh['fsdp'=2,'ctx'=4,'tp'=4] {'fsdp','ctx','tp'}, use_global_device_ids=true, to_apply=%region_25.26 | all-reduce | flops 12288 | bytes 98304 | tf_op jit(solution)/shard_map/psum | solution.py:199
  684.8 13.7 %reduce-scatter.19.cloned.1.call-done = bf16[128,1024]{1,0:T(8,128)(2,1)} async-done(((bf16[1024,1024]{1,0:T(8,128)(2,1)}), bf16[128,1024]{1,0:T(8,128)(2,1)}) %reduce-scatter.19.cloned.1.call-update) | async-done | bytes 262160
  706.1 43.8 %all-gather.23.cloned.1.call-done = bf16[4,256,1024]{2,1,0:T(8,128)(2,1)} async-done(((bf16[1,256,1024]{2,1,0:T(8,128)(2,1)}), bf16[4,256,1024]{2,1,0:T(8,128)(2,1)}) %all-gather.23.cloned.1.call-update) | async-done | bytes 2097168 | tf_op jit(solution)/shard_map/all_gather | solution.py:175
  749.9 4.1 convert_element_type.202
  (150 shorter events, 30.3 us)
Async XLA Ops:
  7.2 29.3 %all-gather.9.cloned.1.call-start = ((), (), s32[]{:S(2)}) async-start(), calls=%async_computation.6 | async-start | bytes 2621440 | tf_op jit(solution)/shard_map/all_gather | solution.py:96
  9.1 81.9 %all-gather.11.cloned.1.call-start = ((), (), s32[]{:S(2)}) async-start(), calls=%async_computation.7 | async-start | bytes 2359296 | tf_op jit(solution)/shard_map/all_gather | solution.py:76
  10.2 0.7 collective-permute-start
  11.6 137.9 %reduce-scatter.11.cloned.1.call-start = ((), (), s32[]{:S(2)}) async-start(), calls=%async_computation.8 | async-start | bytes 2621440 | tf_op jit(solution)/shard_map/reduce_scatter | solution.py:102
  12.4 2.6 collective-permute-start.1
  95.2 9.5 %copy-start.6 = (bf16[1024,256]{0,1:T(8,128)(2,1)}, bf16[1024,256]{0,1:T(8,128)(2,1)S(1)}, u32[]{:S(2)}) copy-start(bf16[1024,256]{0,1:T(8,128)(2,1)S(1)} %get-tuple-element.70) | copy-start | bytes 1572868
  95.2 9.5 %copy-start.13 = (bf16[1024,256]{0,1:T(8,128)(2,1)}, bf16[1024,256]{0,1:T(8,128)(2,1)S(1)}, u32[]{:S(2)}) copy-start(bf16[1024,256]{0,1:T(8,128)(2,1)S(1)} %get-tuple-element.71) | copy-start | bytes 1572868
  112.1 4.2 copy-start.16
  112.1 4.2 copy-start.17
  112.1 37.4 %copy-start.1 = (bf16[4,256,1024]{2,1,0:T(8,128)(2,1)S(1)}, bf16[4,256,1024]{2,1,0:T(8,128)(2,1)}, u32[]{:S(2)}) copy-start(bf16[4,256,1024]{2,1,0:T(8,128)(2,1)} %param.18) | copy-start | bytes 6291460
  112.1 37.4 %copy-start.18 = (f32[1024]{0:T(1024)S(1)}, f32[1024]{0:T(1024)}, u32[]{:S(2)}) copy-start(f32[1024]{0:T(1024)} %param.26) | copy-start | bytes 12292
  112.9 39.3 %copy-start.19 = (f32[1024]{0:T(1024)S(1)}, f32[1024]{0:T(1024)}, u32[]{:S(2)}) copy-start(f32[1024]{0:T(1024)} %param.27) | copy-start | bytes 12292
  112.9 39.3 %copy-start.21 = (f32[1024]{0:T(1024)S(1)}, f32[1024]{0:T(1024)}, u32[]{:S(2)}) copy-start(f32[1024]{0:T(1024)} %param.28) | copy-start | bytes 12292
  116.3 110.3 %all-gather.15.cloned.1.call-start = ((), (), s32[]{:S(2)}) async-start(), calls=%async_computation.10 | async-start | bytes 4718592 | tf_op jit(solution)/shard_map/all_gather | solution.py:76
  116.4 0.7 collective-permute-start.2
  117.9 131.7 %all-gather.13.cloned.1.call-start = ((), (), s32[]{:S(2)}) async-start(), calls=%async_computation.9 | async-start | bytes 2621440 | tf_op jit(solution)/shard_map/all_gather | solution.py:96
  154.4 146.8 %reduce-scatter.13.cloned.1.call-start = ((), (), s32[]{:S(2)}) async-start(), calls=%async_computation.11 | async-start | bytes 2621440 | tf_op jit(solution)/shard_map/reduce_scatter | solution.py:102
  249.6 16.4 %copy-start.25 = (bf16[1024,2048]{1,0:T(8,128)(2,1)S(1)}, bf16[1024,2048]{1,0:T(8,128)(2,1)}, u32[]{:S(2)}) copy-start(bf16[1024,2048]{1,0:T(8,128)(2,1)} %all-gather.15.cloned.1.call-done) | copy-start | bytes 12582916
  264.6 1.3 copy-start.30
  265.9 35.3 %copy-start = (bf16[1,256,1024]{2,1,0:T(8,128)(2,1)S(1)}, bf16[1,256,1024]{2,1,0:T(8,128)(2,1)}, u32[]{:S(2)}) copy-start(bf16[1,256,1024]{2,1,0:T(8,128)(2,1)} %reduce-scatter.11.cloned.1.call-done) | copy-start | bytes 1572868
  265.9 35.3 %copy-start.23 = (f32[1024]{0:T(1024)S(1)}, f32[1024]{0:T(1024)}, u32[]{:S(2)}) copy-start(f32[1024]{0:T(1024)} %param.32) | copy-start | bytes 12292
  269.6 33.6 %copy-start.22 = (f32[1024]{0:T(1024)S(1)}, f32[1024]{0:T(1024)}, u32[]{:S(2)}) copy-start(f32[1024]{0:T(1024)} %param.33) | copy-start | bytes 12292
  269.6 36.6 %copy-start.24 = (f32[1024]{0:T(1024)S(1)}, f32[1024]{0:T(1024)}, u32[]{:S(2)}) copy-start(f32[1024]{0:T(1024)} %param.34) | copy-start | bytes 12292
  269.6 61.6 %all-gather.19.cloned.1.call-start = ((), (), s32[]{:S(2)}) async-start(), calls=%async_computation.13 | async-start | bytes 2621440 | tf_op jit(solution)/shard_map/all_gather | solution.py:96
  301.2 3.6 copy-start.9
  301.2 5.0 copy-start.8
  308.5 67.8 %reduce-scatter.15.cloned.1.call-start = ((), (), s32[]{:S(2)}) async-start(), calls=%async_computation.14 | async-start | bytes 2621440 | tf_op jit(solution)/shard_map/reduce_scatter | solution.py:102
  331.2 9.8 %copy-start.26 = (bf16[1024,2048]{1,0:T(8,128)(2,1)S(1)}, bf16[1024,2048]{1,0:T(8,128)(2,1)}, u32[]{:S(2)}) copy-start(bf16[1024,2048]{1,0:T(8,128)(2,1)} %all-gather.15.cloned.1.call-done) | copy-start | bytes 12582916
  339.7 1.3 copy-start.31
  344.7 61.2 %all-gather.21.cloned.1.call-start = ((), (), s32[]{:S(2)}) async-start(), calls=%async_computation.15 | async-start | bytes 2621440 | tf_op jit(solution)/shard_map/all_gather | solution.py:96
  376.3 5.2 copy-start.2
  376.3 5.2 copy-start.4
  383.2 95.4 %reduce-scatter.17.cloned.1.call-start = ((), (), s32[]{:S(2)}) async-start(), calls=%async_computation.16 | async-start | bytes 2621440 | tf_op jit(solution)/shard_map/reduce_scatter | solution.py:102
  408.3 8.6 %copy-start.14 = (bf16[1024,256]{0,1:T(8,128)(2,1)S(1)}, bf16[1024,256]{0,1:T(8,128)(2,1)}, u32[]{:S(2)}) copy-start(bf16[1024,256]{0,1:T(8,128)(2,1)} %copy-done.13) | copy-start | bytes 1572868
  416.9 26.8 %copy-start.28 = (bf16[4,1024,64]{1,2,0:T(8,128)(2,1)}, bf16[4,1024,64]{1,2,0:T(8,128)(2,1)S(1)}, u32[]{:S(2)}) copy-start(bf16[4,1024,64]{1,2,0:T(8,128)(2,1)S(1)} %get-tuple-element.98) | copy-start | bytes 1572868
  427.6 11.8 %copy-start.7 = (bf16[1024,256]{0,1:T(8,128)(2,1)S(1)}, bf16[1024,256]{0,1:T(8,128)(2,1)}, u32[]{:S(2)}) copy-start(bf16[1024,256]{0,1:T(8,128)(2,1)} %copy-done.6) | copy-start | bytes 1572868
  442.1 1.7 copy-start.20
  447.0 79.7 %all-gather.17.cloned.1.call-start = ((), (), s32[]{:S(2)}) async-start(), calls=%async_computation.12 | async-start | bytes 2621440 | tf_op jit(solution)/shard_map/all_gather | solution.py:147
  447.7 5.0 copy-start.27
  447.7 169.1 %reduce-scatter.21.cloned.1.call-start = ((), (), s32[]{:S(2)}) async-start(), calls=%async_computation.19 | async-start | bytes 4718592
  448.0 4.8 copy-start.32
  464.2 3.4 copy-start.29
  464.2 234.3 %reduce-scatter.19.cloned.1.call-start = ((), (), s32[]{:S(2)}) async-start(), calls=%async_computation.18 | async-start | bytes 2359296
  471.1 55.6 %copy-start.3 = (f32[256,1024]{1,0:T(8,128)S(1)}, f32[256,1024]{1,0:T(8,128)}, u32[]{:S(2)}) copy-start(f32[256,1024]{1,0:T(8,128)} %get-tuple-element.61) | copy-start | bytes 3145732
  473.7 276.2 %all-gather.23.cloned.1.call-start = ((), (), s32[]{:S(2)}) async-start(), calls=%async_computation.17 | async-start | bytes 2621440 | tf_op jit(solution)/shard_map/all_gather | solution.py:175
  618.2 82.8 %collective-permute-start.4 = (bf16[128,2048]{0,1:T(8,128)(2,1)S(1)}, bf16[128,2048]{0,1:T(8,128)(2,1)S(1)}, u32[]{:S(2)}, u32[]{:S(2)}) collective-permute-start(bf16[128,2048]{0,1:T(8,128)(2,1)S(1)} %copy.62), channel_id=1, source_target_pairs={{0,0},{1,4},{2,8},{3,12},{4,1},{5,5},{6,9},{7,13},{8,2},{9,6},{10,... | collective-permute-start | bytes 1572872 | tf_op jit(solution)/shard_map/ppermute | solution.py:80
  699.6 3.4 collective-permute-start.3
  703.0 51.0 %copy-start.5 = (bf16[4,256,1024]{2,1,0:T(8,128)(2,1)S(1)}, bf16[4,256,1024]{2,1,0:T(8,128)(2,1)}, u32[]{:S(2)}) copy-start(bf16[4,256,1024]{2,1,0:T(8,128)(2,1)} %all-gather.17.cloned.1.call-done) | copy-start | bytes 6291460
  (4 other events, 3.4 us)
Sparse Core Ops, SparseCore 0:
  10.2 26.2 all-gather.8
  39.2 51.8 all-gather.10
  116.4 33.0 reduce-scatter.10
  152.2 74.3 all-gather.14
  228.7 20.8 all-gather.12
  269.8 31.3 reduce-scatter.12
  308.6 22.5 all-gather.18
  344.9 31.4 reduce-scatter.14
  383.3 22.5 all-gather.20
  447.1 31.4 reduce-scatter.16
  480.7 45.9 all-gather.16
  530.2 86.6 reduce-scatter.20
  621.4 77.1 reduce-scatter.18
  700.6 49.2 all-gather.22

commit v2 on v1

v2 whole, which is shorter than its diff:
```python
import functools
import math

import jax
import jax.numpy as jnp
from jax import lax
from jax.experimental import pallas as pl
from jax.experimental.pallas import tpu as pltpu
from jax.sharding import PartitionSpec as P

DH = 64
MESH = pl.DeviceIdType.MESH
F32 = jnp.float32
BF16 = jnp.bfloat16
TILE = 256
ROWS = 16
CHUNKS = 2


def dot(left, right):
    return jnp.dot(left, right, preferred_element_type=F32)


def dot_last(left, right):
    return lax.dot_general(left, right, (((1,), (1,)), ((), ())), preferred_element_type=F32)


def dot_first(left, right):
    return lax.dot_general(left, right, (((0,), (0,)), ((), ())), preferred_element_type=F32)


def aligned(index, size):
    return pl.ds(pl.multiple_of(index * size, size), size)


def layer(
    dims,
    lens,
    x_h,
    ct_h,
    wq_h,
    wk_h,
    wv_h,
    wo_h,
    wu_h,
    wd_h,
    bias_h,
    vec,
    res_h,
    gi_h,
    gffn_o,
    gatt_o,
    small_o,
    wqkv,
    wo,
    wu,
    wd,
    z0,
    z1,
    z2,
    z3,
    x_tok,
    nl,
    dl2,
    dl1,
    qs,
    kk,
    vv,
    kt,
    vt,
    att,
    datt,
    ot,
    lse,
    act,
    dg,
    dpl,
    dqkv,
    dk_acc,
    dv_acc,
    ps,
    pr,
    ysend,
    yrecv,
    acc_y,
    acc_o,
    xh1,
    rstd1,
    dres,
    res_s,
    gi_s,
    ct_s,
    bias,
    gwd,
    gwu,
    gqkv,
    gwo,
    xg_d,
    xg_u,
    xg_q,
    xg_o,
    zg_d,
    zg_u,
    zg_q,
    zg_o,
    sums,
    sm,
    smz,
    smx,
    smc,
    loc_sem,
    bias_s,
    bias_r,
    wz_s,
    wz_r,
    wy_s,
    wy_r,
    wx_s,
    wx_r,
    ag_s,
    ag_r,
    rs_s,
    rs_r,
    ry_s,
    ry_r,
    out_s,
    out_r,
    gx_s,
    gx_r,
    gz_s,
    gz_r,
    sm_s,
    sm_r,
):
    nf, nc, nt = dims
    f = lax.axis_index("fsdp")
    c = lax.axis_index("ctx")
    t = lax.axis_index("tp")
    yi, ki = c // 2, lax.rem(c, 2)
    c_sib = yi * 2 + (1 - ki)
    c_y = (1 - yi) * 2 + ki
    c_ysib = (1 - yi) * 2 + (1 - ki)
    seq, width = ct_s.shape
    tok = x_tok.shape[0]
    rows_w = z0.shape[1]
    hid = wo.shape[1]
    ff = wu.shape[1]
    heads = hid // DH
    scale = 1.0 / math.sqrt(DH)
    chunk = seq // CHUNKS
    sib = (f, c_sib, t)
    ypeer = (f, c_y, t)
    length = lens[t]

    def remote(src, dst, ssem, rsem, dev):
        return pltpu.make_async_remote_copy(
            src_ref=src, dst_ref=dst, send_sem=ssem, recv_sem=rsem, device_id=dev, device_id_type=MESH
        )

    bar = pltpu.get_barrier_semaphore()
    for dc in range(nc):
        for dt in range(nt):
            if dc or dt:
                pl.semaphore_signal(
                    bar,
                    inc=1,
                    device_id=(f, lax.rem(c + dc, nc), lax.rem(t + dt, nt)),
                    device_id_type=MESH,
                )
    for df in range(1, nf):
        pl.semaphore_signal(bar, inc=1, device_id=(lax.rem(f + df, nf), c, t), device_id_type=MESH)
    pl.semaphore_wait(bar, nc * nt - 1 + nf - 1)

    groups = (
        ((wq_h, wk_h, wv_h), z0, wqkv),
        ((wo_h,), z1, wo),
        ((wu_h,), z2, wu),
        ((wd_h,), z3, wd),
    )

    def own_rows(cc):
        return aligned(f * nc + cc, rows_w)

    def w_start(g):
        srcs, stage, _ = groups[g]
        for k, src in enumerate(srcs):
            cols = pl.ds(k * src.shape[1], src.shape[1])
            pltpu.make_async_copy(src, stage.at[t, :, cols], wz_r.at[g, 0]).start()
            for j in range(1, nt):
                remote(
                    src,
                    stage.at[t, :, cols],
                    wz_s.at[g, j],
                    wz_r.at[g, j],
                    (f, c, lax.rem(t + j, nt)),
                ).start()

    def w_cross(g, j):
        _, stage, final = groups[g]
        ts = lax.rem(t + nt - j, nt)
        if j == 0:
            pltpu.make_async_copy(stage.at[ts], stage.at[ts], wz_r.at[g, 0]).wait()
        else:
            remote(stage.at[ts], stage.at[ts], wz_s.at[g, j], wz_r.at[g, j], (f, c, ts)).wait_recv()

        @pl.when(ts == c)
        def _():
            pltpu.make_async_copy(stage.at[ts], final.at[own_rows(c)], wy_r.at[g, c]).start()

        @pl.when(ts != c)
        def _():
            remote(
                stage.at[ts], final.at[own_rows(c)], wy_s.at[g, j], wy_r.at[g, c], (f, ts, t)
            ).start()

    def w_spread(g, i):
        _, _, final = groups[g]
        cc = lax.rem(c + i, nc)
        if i == 0:
            pltpu.make_async_copy(
                final.at[own_rows(cc)], final.at[own_rows(cc)], wy_r.at[g, cc]
            ).wait()
        else:
            remote(
                final.at[own_rows(cc)], final.at[own_rows(cc)], wy_s.at[g, 0], wy_r.at[g, cc], (f, cc, t)
            ).wait_recv()
        for df in range(1, nf):
            remote(
                final.at[own_rows(cc)],
                final.at[own_rows(cc)],
                wx_s.at[g, df],
                wx_r.at[g, df],
                (lax.rem(f + df, nf), c, t),
            ).start()

    def w_wait(g):
        _, _, final = groups[g]
        for df in range(1, nf):
            fs = lax.rem(f + nf - df, nf)
            part = final.at[aligned(fs, nc * rows_w)]
            remote(part, part, wx_s.at[g, df], wx_r.at[g, df], (fs, c, t)).wait_recv()

    def w_finish(g):
        _, stage, final = groups[g]
        for j in range(1, nt):
            remote(
                stage.at[0], stage.at[0], wz_s.at[g, j], wz_r.at[g, j], (f, c, lax.rem(t + j, nt))
            ).wait_send()
        for j in range(nt):
            ts = lax.rem(t + nt - j, nt)

            @pl.when(ts != c)
            def _():
                remote(
                    stage.at[ts], final.at[own_rows(c)], wy_s.at[g, j], wy_r.at[g, c], (f, ts, t)
                ).wait_send()

        for df in range(1, nf):
            part = final.at[aligned(f, nc * rows_w)]
            remote(
                part, part, wx_s.at[g, df], wx_r.at[g, df], (lax.rem(f + df, nf), c, t)
            ).wait_send()

    def part_of(buf, cc, k):
        return buf.at[pl.ds(pl.multiple_of(cc * seq + k * chunk, chunk), chunk)]

    def ag_copy(buf, a, k, cc, way, dev):
        part = part_of(buf, cc, k)
        return remote(part, part, ag_s.at[a, way, k], ag_r.at[a, way, k], dev)

    def ag_send(buf, a, k):
        ag_copy(buf, a, k, c, 1, ypeer).start()
        ag_copy(buf, a, k, c, 0, sib).start()

    def ag_pass(buf, a, k):
        ag_copy(buf, a, k, c_y, 1, ypeer).wait_recv()
        ag_copy(buf, a, k, c_y, 2, sib).start()

    def ag_wait(buf, a, k, way):
        ag_copy(buf, a, k, c_sib if way == 0 else c_ysib, way, sib).wait_recv()

    def ag_finish(buf, a):
        for k in range(CHUNKS):
            ag_copy(buf, a, k, c, 0, sib).wait_send()
            ag_copy(buf, a, k, c, 1, ypeer).wait_send()
            ag_copy(buf, a, k, c_y, 2, sib).wait_send()

    tiles = width // TILE

    def rs_copy(o, slot):
        return remote(ps.at[slot], pr.at[slot], rs_s.at[o, slot], rs_r.at[o, slot], sib)

    def ry_copy(o, k):
        rows = pl.ds(k * chunk, chunk)
        return remote(ysend.at[rows], yrecv.at[rows], ry_s.at[o, k], ry_r.at[o, k], ypeer)

    def rs_sib(o, slot, produce):
        if o:
            rs_copy(o - 1, slot).wait_send()

        def tile(n, _):
            ps[slot, :, aligned(n, TILE)] = produce(n).astype(BF16)
            return 0

        lax.fori_loop(0, tiles, tile, 0)
        rs_copy(o, slot).start()

    def rs_y(o, produce):
        def tile(n, _):
            acc_y[:, aligned(n, TILE)] = produce(n)
            return 0

        lax.fori_loop(0, tiles, tile, 0)
        rs_copy(o, 0).wait_recv()
        for k in range(CHUNKS):
            if o:
                ry_copy(o - 1, k).wait_send()

            def add(i, _, k=k):
                rows = pl.ds(pl.multiple_of(k * chunk + i * ROWS, ROWS), ROWS)
                ysend[rows] = (acc_y[rows] + pr[0, rows].astype(F32)).astype(BF16)
                return 0

            lax.fori_loop(0, chunk // ROWS, add, 0)
            ry_copy(o, k).start()

    def rs_own(o, produce):
        def tile(n, _):
            acc_o[:, aligned(n, TILE)] = produce(n)
            return 0

        lax.fori_loop(0, tiles, tile, 0)

    def rs_row(rows):
        return acc_o[rows] + pr[1, rows].astype(F32) + yrecv[rows].astype(F32)

    def rs_rows(o, k, body):
        ry_copy(o, k).wait_recv()

        def step(i, _):
            body(pl.ds(pl.multiple_of(k * chunk + i * ROWS, ROWS), ROWS), i)
            return 0

        lax.fori_loop(0, chunk // ROWS, step, 0)

    def add_sum(k, value):
        half = value[0:8]
        for r in range(8, ROWS, 8):
            half = half + value[r : r + 8]
        sums[k] = sums[k] + half

    def mean(value):
        return jnp.sum(value, -1, keepdims=True) * (1.0 / width)

    w_start(0)
    pltpu.make_async_copy(x_h.at[t], x_tok.at[aligned(c, seq)], loc_sem.at[0]).start()
    pltpu.make_async_copy(ct_h.at[t], ct_s, loc_sem.at[1]).start()

    @pl.when(t == c)
    def _():
        pltpu.make_async_copy(bias_h, bias, loc_sem.at[2]).start()
        for j in range(1, nt):
            remote(bias_h, bias, bias_s.at[j], bias_r.at[0], (f, c, lax.rem(t + j, nt))).start()

    pltpu.make_async_copy(x_h.at[t], x_tok.at[aligned(c, seq)], loc_sem.at[0]).wait()
    for k in range(CHUNKS):
        ag_send(x_tok, 0, k)
    w_cross(0, 0)
    sums[...] = jnp.zeros_like(sums)
    for k in range(CHUNKS):
        ag_pass(x_tok, 0, k)
    for j in range(1, nt):
        w_cross(0, j)
    for g in range(1, 4):
        w_start(g)

    @pl.when(t == c)
    def _():
        pltpu.make_async_copy(bias_h, bias, loc_sem.at[2]).wait()

    @pl.when(t != c)
    def _():
        remote(bias_h, bias, bias_s.at[0], bias_r.at[0], (f, c, c)).wait_recv()

    for i in range(nc):
        w_spread(0, i)
    for k in range(CHUNKS):
        ag_wait(x_tok, 0, k, 0)
        ag_wait(x_tok, 0, k, 2)
    for g in range(1, 4):
        w_cross(g, 0)
    w_wait(0)

    def project(b, _):
        rows = aligned(b, seq)
        xb = x_tok[rows]
        qv = dot(xb, wqkv[:, 0:hid]) + bias[0:1, 0:hid]
        qs[rows] = (qv * scale).astype(BF16)
        kb = dot(xb, wqkv[:, hid : 2 * hid])
        kk[rows] = kb.astype(BF16)
        kt[:, rows] = kb.T.astype(BF16)
        vb = dot(xb, wqkv[:, 2 * hid : 3 * hid]) + bias[0:1, hid : 2 * hid]
        vv[rows] = vb.astype(BF16)
        vt[:, rows] = vb.T.astype(BF16)
        return 0

    lax.fori_loop(0, nc, project, 0)

    lane = lax.broadcasted_iota(jnp.int32, (seq, hid), 1)

    def head_part(value, h):
        inside = (lane >= h * DH) & (lane < (h + 1) * DH)
        return jnp.where(inside, value, jnp.zeros_like(value))

    def masked_scores(qm):
        s = dot_last(kk[...], qm)
        key = lax.broadcasted_iota(jnp.int32, s.shape, 0)
        return jnp.where(key < length, s, -1e30)

    def attend(b):
        rows = aligned(b, seq)
        qb = qs[rows]

        def head(h, _):
            s = masked_scores(head_part(qb, h))
            top = jnp.max(s, 0, keepdims=True)
            e = jnp.exp(s - top)
            total = jnp.sum(e, 0, keepdims=True)
            hrows = aligned(h, DH)
            ot[hrows] = dot(vt[hrows], e.astype(BF16)) / total
            lse[h, :, rows] = top + jnp.log(total)
            return 0

        lax.fori_loop(0, heads, head, 0)
        att[rows] = ot[...].T.astype(BF16)

    def out_proj(b):
        ab = att[aligned(b, seq)]
        return lambda n: dot_last(ab, wo[aligned(n, TILE)])

    attend(c_ysib)
    for j in range(1, nt):
        w_cross(1, j)
    attend(c_y)
    for i in range(nc):
        w_spread(1, i)
    w_wait(1)
    rs_sib(0, 0, out_proj(c_ysib))
    rs_y(0, out_proj(c_y))
    for j in range(1, nt):
        w_cross(2, j)
    attend(c_sib)
    rs_sib(0, 1, out_proj(c_sib))
    for i in range(nc):
        w_spread(2, i)
    attend(c)
    rs_own(0, out_proj(c))
    rs_copy(0, 1).wait_recv()

    b_out, gain1, shift1 = vec[0:1], vec[1:2], vec[2:3]
    b_down, gain2, shift2 = vec[3:4], vec[4:5], vec[5:6]
    own = c * seq

    def own_slice(rows):
        return pl.ds(pl.multiple_of(own + rows.start, ROWS), ROWS)

    def norm1(rows, i):
        h = x_tok[own_slice(rows)].astype(F32) + rs_row(rows) + b_out
        cen = h - mean(h)
        inv = lax.rsqrt(mean(cen * cen) + 1e-5)
        xh = cen * inv
        xh1[rows] = xh
        rstd1[rows] = jnp.broadcast_to(inv, (ROWS, 128))
        nl[own_slice(rows)] = (xh * gain1 + shift1).astype(BF16)

    for k in range(CHUNKS):
        rs_rows(0, k, norm1)
        ag_send(nl, 1, k)
    for j in range(1, nt):
        w_cross(3, j)
    w_wait(2)

    def up(b):
        rows = aligned(b, seq)
        nb = nl[rows]

        def tile(n, _):
            cols = aligned(n, TILE)
            v = dot(nb, wu[:, cols]) + bias[0:1, pl.ds(pl.multiple_of(2 * hid + n * TILE, 128), TILE)]
            cdf = 0.5 * (1.0 + lax.erf(v * math.sqrt(0.5)))
            act[rows, cols] = (v * cdf).astype(BF16)
            pdf = jnp.exp(-0.5 * v * v) * (1.0 / math.sqrt(2.0 * math.pi))
            dg[rows, cols] = (cdf + v * pdf).astype(BF16)
            return 0

        lax.fori_loop(0, ff // TILE, tile, 0)

    def down(b):
        ab = act[aligned(b, seq)]
        return lambda n: dot_last(ab, wd[aligned(n, TILE)])

    up(c)
    for i in range(nc):
        w_spread(3, i)
    for k in range(CHUNKS):
        ag_wait(nl, 1, k, 0)
    up(c_sib)
    for k in range(CHUNKS):
        ag_pass(nl, 1, k)
    w_wait(3)
    rs_sib(1, 1, down(c_sib))
    rs_own(1, down(c))
    up(c_y)
    for k in range(CHUNKS):
        ag_wait(nl, 1, k, 2)
    up(c_ysib)
    rs_sib(1, 0, down(c_ysib))
    rs_y(1, down(c_y))
    rs_copy(1, 1).wait_recv()
    pltpu.make_async_copy(ct_h.at[t], ct_s, loc_sem.at[1]).wait()

    def norm2(rows, i):
        h = xh1[rows] * gain1 + shift1 + rs_row(rows) + b_down
        cen = h - mean(h)
        inv = lax.rsqrt(mean(cen * cen) + 1e-5)
        xh = cen * inv
        res_s[rows] = (xh * gain2 + shift2).astype(BF16)
        pos = own + rows.start + lax.broadcasted_iota(jnp.int32, (ROWS, width), 0)
        top = jnp.where(pos < length, ct_s[rows].astype(F32), 0.0)
        add_sum(4, top * xh)
        add_sum(5, top)
        gy = top * gain2
        dr = (gy - mean(gy) - xh * mean(gy * xh)) * inv
        add_sum(3, dr)
        dres[rows] = dr
        dl2[own_slice(rows)] = dr.astype(BF16)

    for k in range(CHUNKS):
        rs_rows(1, k, norm2)
        ag_send(dl2, 2, k)

    def spread(share, out, o):
        pltpu.make_async_copy(share, out.at[t], out_r.at[o, 0]).start()
        for j in range(1, nt):
            remote(
                share, out.at[t], out_s.at[o, j], out_r.at[o, j], (f, c, lax.rem(t + j, nt))
            ).start()

    def spread_wait(share, out, o):
        pltpu.make_async_copy(share, out.at[t], out_r.at[o, 0]).wait()
        for j in range(1, nt):
            ts = lax.rem(t + nt - j, nt)
            remote(share, out.at[ts], out_s.at[o, j], out_r.at[o, j], (f, c, ts)).wait_recv()
            remote(
                share, out.at[t], out_s.at[o, j], out_r.at[o, j], (f, c, lax.rem(t + j, nt))
            ).wait_send()

    spread(res_s, res_h, 0)

    def back(b):
        rows = aligned(b, seq)
        db = dl2[rows]

        def tile(n, _):
            cols = aligned(n, TILE)
            dp = (dot(db, wd[:, cols]) * dg[rows, cols].astype(F32)).astype(BF16)
            dpl[rows, cols] = dp
            dpf = dp.astype(F32)
            sums[6, :, cols] = sums[6, :, cols] + jnp.sum(dpf.reshape(seq // 8, 8, TILE), 0)
            return 0

        lax.fori_loop(0, ff // TILE, tile, 0)

    def up_back(b):
        pb = dpl[aligned(b, seq)]
        return lambda n: dot_last(pb, wu[aligned(n, TILE)])

    def weight_grad(dst, left, right):
        def step(m, _):
            rows = aligned(m, TILE)
            dst[rows] = dot_first(left[:, rows], right[...]).astype(BF16)
            return 0

        lax.fori_loop(0, width // TILE, step, 0)

    grads = ((gwd, xg_d, zg_d), (gwu, xg_u, zg_u), (gwo, xg_o, zg_o), (gqkv, xg_q, zg_q))
    part_rows = nc * rows_w

    def gx_copy(g, df, dev_f):
        buf, got, _ = grads[g]
        return remote(
            buf.at[aligned(dev_f, part_rows)],
            got.at[df - 1],
            gx_s.at[g, df],
            gx_r.at[g, df],
            (dev_f, c, t),
        )

    def g_start(g):
        for df in range(1, nf):
            gx_copy(g, df, lax.rem(f + df, nf)).start()

    def gz_copy(g, dc):
        buf, _, got = grads[g]
        cc = lax.rem(c + dc, nc)
        return remote(buf.at[own_rows(cc)], got.at[t], gz_s.at[g, dc], gz_r.at[g, t], (f, cc, c))

    def g_cross(g):
        buf, got, _ = grads[g]
        for df in range(1, nf):
            gx_copy(g, df, lax.rem(f + nf - df, nf)).wait_recv()

        def add(i, _):
            rows = pl.ds(pl.multiple_of(f * part_rows + i * ROWS, ROWS), ROWS)
            total = buf[rows].astype(F32)
            for df in range(1, nf):
                total = total + got[df - 1, pl.ds(pl.multiple_of(i * ROWS, ROWS), ROWS)].astype(F32)
            buf[rows] = total.astype(BF16)
            return 0

        lax.fori_loop(0, part_rows // ROWS, add, 0)
        for dc in range(1, nc):
            gz_copy(g, dc).start()

        @pl.when(t != c)
        def _():
            gz_copy(g, 0).start()

        @pl.when(t == c)
        def _():
            pltpu.make_async_copy(
                buf.at[own_rows(c)], grads[g][2].at[t], gz_r.at[g, t]
            ).start()

    def g_out(g, store):
        _, _, got = grads[g]
        for s in range(nt):
            remote(got.at[s], got.at[s], gz_s.at[g, 0], gz_r.at[g, s], (f, t, s)).wait_recv()

        def add(i, _):
            rows = pl.ds(pl.multiple_of(i * ROWS, ROWS), ROWS)
            total = got[0, rows].astype(F32)
            for s in range(1, nt):
                total = total + got[s, rows].astype(F32)
            store(rows, total)
            return 0

        lax.fori_loop(0, rows_w // ROWS, add, 0)

    def g_finish(g):
        for df in range(1, nf):
            gx_copy(g, df, lax.rem(f + df, nf)).wait_send()
        for dc in range(1, nc):
            gz_copy(g, dc).wait_send()

        @pl.when(t != c)
        def _():
            gz_copy(g, 0).wait_send()

    back(c)
    for k in range(CHUNKS):
        ag_wait(dl2, 2, k, 0)
    back(c_sib)
    rs_sib(2, 1, up_back(c_sib))
    rs_own(2, up_back(c))
    for k in range(CHUNKS):
        ag_pass(dl2, 2, k)
    back(c_y)
    for k in range(CHUNKS):
        ag_wait(dl2, 2, k, 2)
    back(c_ysib)
    rs_sib(2, 0, up_back(c_ysib))
    rs_y(2, up_back(c_y))
    weight_grad(gwd, dl2, act)
    g_start(0)
    rs_copy(2, 1).wait_recv()

    def norm1_back(rows, i):
        dn = dres[rows] + rs_row(rows)
        xh = xh1[rows]
        add_sum(1, dn * xh)
        add_sum(2, dn)
        gy = dn * gain1
        dr = (gy - mean(gy) - xh * mean(gy * xh)) * rstd1[rows, 0:1]
        add_sum(0, dr)
        dres[rows] = dr
        dl1[own_slice(rows)] = dr.astype(BF16)

    for k in range(CHUNKS):
        rs_rows(2, k, norm1_back)
        ag_send(dl1, 3, k)
    weight_grad(gwu, nl, dpl)
    g_start(1)

    dk_acc[...] = jnp.zeros_like(dk_acc)
    dv_acc[...] = jnp.zeros_like(dv_acc)

    def attend_back(b):
        rows = aligned(b, seq)
        datt[rows] = dot(dl1[rows], wo[...]).astype(BF16)
        qb = qs[rows]
        db = datt[rows]

        def head(h, _):
            qm = head_part(qb, h)
            dm = head_part(db, h)
            p = jnp.exp(masked_scores(qm) - lse[h, :, rows])
            dv_acc[...] += dot(p.astype(BF16), dm)
            pd = p * dot_last(vv[...], dm)
            delta = jnp.sum(pd, 0, keepdims=True)
            ds = (pd - p * delta).astype(BF16)
            dk_acc[...] += dot(ds, qm)
            hrows = aligned(h, DH)
            ot[hrows] = dot(kt[hrows], ds)
            return 0

        lax.fori_loop(0, heads, head, 0)
        dq = (ot[...].T * scale).astype(BF16)
        dqkv[rows, 0:hid] = dq
        dqf = dq.astype(F32)
        sums[7, :, 0:hid] = sums[7, :, 0:hid] + jnp.sum(dqf.reshape(seq // 8, 8, hid), 0)

    attend_back(c)
    for k in range(CHUNKS):
        ag_wait(dl1, 3, k, 0)
    for k in range(CHUNKS):
        ag_pass(dl1, 3, k)
    attend_back(c_sib)
    g_cross(0)
    attend_back(c_y)
    for k in range(CHUNKS):
        ag_wait(dl1, 3, k, 2)
    weight_grad(gwo, dl1, att)
    g_start(2)
    attend_back(c_ysib)
    g_cross(1)

    def finish_kv(b, _):
        rows = aligned(b, seq)
        dqkv[rows, hid : 2 * hid] = dk_acc[rows].astype(BF16)
        dvb = dv_acc[rows].astype(BF16)
        dqkv[rows, 2 * hid : 3 * hid] = dvb
        sums[7, :, hid : 2 * hid] = sums[7, :, hid : 2 * hid] + jnp.sum(
            dvb.astype(F32).reshape(seq // 8, 8, hid), 0
        )
        return 0

    lax.fori_loop(0, nc, finish_kv, 0)

    def in_back(b):
        qb = dqkv[aligned(b, seq)]
        return lambda n: dot_last(qb, wqkv[aligned(n, TILE)])

    rs_sib(3, 0, in_back(c_ysib))
    rs_y(3, in_back(c_y))
    rs_sib(3, 1, in_back(c_sib))
    rs_own(3, in_back(c))
    weight_grad(gqkv, x_tok, dqkv)
    g_start(3)
    sm[...] = jnp.sum(sums[...], 1)

    def sm_copy(stage, j, src, dst, dev):
        return remote(src, dst, sm_s.at[stage, j], sm_r.at[stage, j], dev)

    for j in range(1, nt):
        sm_copy(0, j, sm, smz.at[j], (f, c, lax.rem(t + j, nt))).start()
    rs_copy(3, 1).wait_recv()

    def grad_in(rows, i):
        gi_s[rows] = (dres[rows] + rs_row(rows)).astype(BF16)

    for k in range(CHUNKS):
        rs_rows(3, k, grad_in)
    spread(gi_s, gi_h, 1)
    g_cross(2)
    total = sm[...]
    for j in range(1, nt):
        sm_copy(0, j, sm, smz.at[j], (f, c, lax.rem(t + nt - j, nt))).wait_recv()
        total = total + smz[j]
    smz[0] = total
    for df in range(1, nf):
        sm_copy(1, df, smz.at[0], smx.at[df], (lax.rem(f + df, nf), c, t)).start()
    g_cross(3)

    def store_at(out, base):
        def store(rows, value):
            out[rows, base : base + value.shape[1]] = value

        return store

    for df in range(1, nf):
        sm_copy(1, df, smz.at[0], smx.at[df], (lax.rem(f + nf - df, nf), c, t)).wait_recv()
        total = total + smx[df]
    smx[0] = total
    for dc in range(1, nc):
        sm_copy(2, dc, smx.at[0], smc.at[c], (f, lax.rem(c + dc, nc), t)).start()
    smc[c] = total
    g_out(0, store_at(gffn_o, ff))
    g_out(1, store_at(gffn_o, 0))
    g_out(2, store_at(gatt_o, 3 * hid))
    for dc in range(1, nc):
        cs = lax.rem(c + nc - dc, nc)
        sm_copy(2, dc, smx.at[0], smc.at[cs], (f, cs, t)).wait_recv()
    whole = smc[0]
    for s in range(1, nc):
        whole = whole + smc[s]
    small_o[0:6] = whole[0:6]
    small_o[6:8] = smc[t, 6:8]
    g_out(3, store_at(gatt_o, 0))
    spread_wait(res_s, res_h, 0)
    spread_wait(gi_s, gi_h, 1)

    for g in range(4):
        w_finish(g)
        g_finish(g)
    for a, buf in enumerate((x_tok, nl, dl2, dl1)):
        ag_finish(buf, a)
    rs_copy(3, 0).wait_send()
    rs_copy(3, 1).wait_send()
    for k in range(CHUNKS):
        ry_copy(3, k).wait_send()
    for j in range(1, nt):
        sm_copy(0, j, sm, smz.at[j], (f, c, lax.rem(t + j, nt))).wait_send()
    for df in range(1, nf):
        sm_copy(1, df, smz.at[0], smx.at[df], (lax.rem(f + df, nf), c, t)).wait_send()
    for dc in range(1, nc):
        sm_copy(2, dc, smx.at[0], smc.at[c], (f, lax.rem(c + dc, nc), t)).wait_send()

    @pl.when(t == c)
    def _():
        for j in range(1, nt):
            remote(
                bias_h, bias, bias_s.at[j], bias_r.at[0], (f, c, lax.rem(t + j, nt))
            ).wait_send()


def shards(
    dims,
    inputs,
    lengths,
    w_query,
    w_key,
    w_value,
    b_query,
    b_value,
    w_out,
    b_out,
    gain_attn,
    shift_attn,
    w_up,
    b_up,
    w_down,
    b_down,
    gain_ffn,
    shift_ffn,
    cotangent,
):
    nf, nc, nt = dims
    seq_dev, seq, width = inputs.shape
    rows_w, hid = w_query.shape
    ff = w_up.shape[1]
    assert nc == 4 and nt == nc and seq_dev == nt and ff == width
    tok = seq * nc
    heads = hid // DH
    part = nc * rows_w
    bias = jnp.broadcast_to(jnp.concatenate([b_query, b_value, b_up])[None], (8, 2 * hid + ff))
    zero = jnp.zeros_like(b_out)
    vec = jnp.stack([b_out, gain_attn, shift_attn, b_down, gain_ffn, shift_ffn, zero, zero])
    hbm = pl.BlockSpec(memory_space=pl.ANY)
    vmem = pl.BlockSpec(memory_space=pltpu.VMEM)
    smem = pl.BlockSpec(memory_space=pltpu.SMEM)

    def vb(*shape):
        return pltpu.VMEM(shape, BF16)

    def vf(*shape):
        return pltpu.VMEM(shape, F32)

    def sem(*shape):
        return pltpu.SemaphoreType.DMA(shape)

    result, grad_in, g_ffn, g_att, small = pl.pallas_call(
        functools.partial(layer, dims),
        out_shape=(
            jax.ShapeDtypeStruct((nt, seq, width), BF16),
            jax.ShapeDtypeStruct((nt, seq, width), BF16),
            jax.ShapeDtypeStruct((rows_w, 2 * ff), F32),
            jax.ShapeDtypeStruct((rows_w, 4 * hid), F32),
            jax.ShapeDtypeStruct((8, width), F32),
        ),
        in_specs=[smem] + [hbm] * 9 + [vmem],
        out_specs=(hbm, hbm, vmem, vmem, vmem),
        scratch_shapes=[
            vb(width, 3 * hid),
            vb(width, hid),
            vb(width, ff),
            vb(width, ff),
            vb(nt, rows_w, 3 * hid),
            vb(nt, rows_w, hid),
            vb(nt, rows_w, ff),
            vb(nt, rows_w, ff),
            vb(tok, width),
            vb(tok, width),
            vb(tok, width),
            vb(tok, width),
            vb(tok, hid),
            vb(tok, hid),
            vb(tok, hid),
            vb(hid, tok),
            vb(hid, tok),
            vb(tok, hid),
            vb(tok, hid),
            vf(hid, seq),
            vf(heads, 1, tok),
            vb(tok, ff),
            vb(tok, ff),
            vb(tok, ff),
            vb(tok, 3 * hid),
            vf(tok, hid),
            vf(tok, hid),
            vb(2, seq, width),
            vb(2, seq, width),
            vb(seq, width),
            vb(seq, width),
            vf(seq, width),
            vf(seq, width),
            vf(seq, width),
            vf(seq, 128),
            vf(seq, width),
            vb(seq, width),
            vb(seq, width),
            vb(seq, width),
            vf(8, 2 * hid + ff),
            vb(width, ff),
            vb(width, ff),
            vb(width, 3 * hid),
            vb(width, hid),
            vb(nf - 1, part, ff),
            vb(nf - 1, part, ff),
            vb(nf - 1, part, 3 * hid),
            vb(nf - 1, part, hid),
            vb(nt, rows_w, ff),
            vb(nt, rows_w, ff),
            vb(nt, rows_w, 3 * hid),
            vb(nt, rows_w, hid),
            vf(8, 8, width),
            vf(8, width),
            vf(nt, 8, width),
            vf(nf, 8, width),
            vf(nc, 8, width),
            sem(3),
            sem(nt),
            sem(1),
            sem(4, nt),
            sem(4, nt),
            sem(4, nt),
            sem(4, nc),
            sem(4, nf),
            sem(4, nf),
            sem(4, 3, CHUNKS),
            sem(4, 3, CHUNKS),
            sem(4, 2),
            sem(4, 2),
            sem(4, CHUNKS),
            sem(4, CHUNKS),
            sem(2, nt),
            sem(2, nt),
            sem(4, nf),
            sem(4, nf),
            sem(4, nc),
            sem(4, nt),
            sem(3, max(nf, nc)),
            sem(3, max(nf, nc)),
        ],
        compiler_params=pltpu.CompilerParams(
            collective_id=0, has_side_effects=True, vmem_limit_bytes=63 << 20
        ),
    )(lengths, inputs, cotangent, w_query, w_key, w_value, w_out, w_up, w_down, bias, vec)
    return (
        result,
        grad_in.astype(F32),
        g_att[:, :hid],
        g_att[:, hid : 2 * hid],
        g_att[:, 2 * hid : 3 * hid],
        small[7, :hid],
        small[7, hid : 2 * hid],
        g_att[:, 3 * hid :],
        small[0],
        small[1],
        small[2],
        g_ffn[:, :ff],
        small[6, :ff],
        g_ffn[:, ff:],
        small[3],
        small[4],
        small[5],
    )


def solution(mesh):
    weight = P(("fsdp", "ctx"), "tp")
    acts = P("fsdp", "ctx", None)
    dims = tuple(mesh.shape[a] for a in ("fsdp", "ctx", "tp"))
    return jax.shard_map(
        functools.partial(shards, dims),
        mesh=mesh,
        in_specs=(
            acts,
            P("fsdp"),
            weight,
            weight,
            weight,
            P("tp"),
            P("tp"),
            weight,
            P(),
            P(),
            P(),
            weight,
            P("tp"),
            weight,
            P(),
            P(),
            P(),
            acts,
        ),
        out_specs=(
            acts,
            acts,
            weight,
            weight,
            weight,
            P("tp"),
            P("tp"),
            weight,
            P(),
            P(),
            P(),
            weight,
            P("tp"),
            weight,
            P(),
            P(),
            P(),
        ),
        check_vma=False,
    )
```

time: 770 us -> 395 us (0.51)
  waiting for transfers between devices: 508 us -> 0 us
  Pallas kernels: 0 us -> 380 us
  matrix products: 96.9 us -> 0 us
  blocking collectives: 65.3 us -> 0 us
  other arithmetic: 43 us -> 3.2 us
  local copies, waits for them, and re-layouts: 28.8 us -> 10.8 us
  between operations: 14.7 us -> 0.68 us
    pallas_call x0 -> x1, Pallas kernels: none -> 380 us  [shards(): pl.pallas_call(functools.partial(layer, dims), out_shape=(jax.ShapeDtypeS...]
    all_gather x8 -> x0, waiting for transfers between devices: 305 us -> none  [the longest x2 127 us: gather_cols(): return lax.all_gather(moved, ('fsdp', 'tp'), axis=0, tiled=True)]
    unnamed x16 -> x0, waiting for transfers between devices: 104 us -> none
    reduce_scatter x4 -> x0, waiting for transfers between devices: 98.7 us -> none  [to_share(): lax.psum_scatter(low(rows).reshape(per_tp, seq_full, -1), 'ctx', scatter_...]
    dot_general x17 -> x0, matrix products: 87.5 us -> none  [the longest x4 29.8 us: dot(): return jnp.dot(left, right, preferred_element_type=jnp.float32)]
    psum x1 -> x0, blocking collectives: 65.3 us -> none  [shards(): lax.psum(jnp.concatenate([blocks.reshape(-1), whole.reshape(-1)]), ('fsdp...]
    convert_element_type x8 -> x1, other arithmetic: 25 us -> 2.48 us  [shards(): grad_in.astype(F32)]
    unnamed x77 -> x5, local copies, waits for them, and re-layouts: 23.8 us -> 1.33 us
  transfers between devices with their start and end apart: 19 -> 0, of which waited for: 14 -> 0; matrix products, arithmetic and copies ran while one was open for 6% -> 0% of each run, Pallas kernels for 0% -> 0%
where the time goes in v2:
time: 395 us
  Pallas kernels  380 us (96%)
  local copies, waits for them, and re-layouts  10.8 us (3%)
    pallas_call x1, Pallas kernels, shards(): pl.pallas_call(functools.partial(layer, dims), out_shape=(jax.ShapeDtypeS...  380 us

profile of v2, /device:TPU:0, one launch (start us, length us, event | category | flops | bytes accessed | tf_op | source)
XLA Modules:
  0.0 394.5 jit_solution(14364045944436318425)
XLA Ops:
  0.7 0.7 pad_maximum_fusion
  1.4 1.4 stack.31.vec
  2.8 0.6 broadcast_in_dim.2.bias_h
  3.4 379.9 %shard_map.305 = (bf16[4,256,1024]{2,1,0:T(8,128)(2,1)}, bf16[4,256,1024]{2,1,0:T(8,128)(2,1)}, f32[128,2048]{1,0:T(8,128)}, f32[128,1024]{1,0:T(8,128)}, f32[8,1024]{1,0:T(8,128)}) custom-call(s32[4]{0:T(128)} %lens.1, bf16[4,256,1024]{2,1,0:T(8,128)(2,1)} %x_h.1, bf16[4,256,1024]{2,1,0:T(8,128)(2,1)} %ct_h.1, bf16[128,256]{1,0:T(8,128)(2,1)} %wq_h.1, ...), custom_call_target="tpu_custom_call" | custom-call | tf_op jit(solution)/shard_map/pallas_call | solution.py:882
  383.3 0.0 copy-start
  383.4 1.4 fusion.3
  384.8 1.8 fusion.2
  386.6 1.9 fusion.1
  388.4 2.3 fusion
  390.7 0.0 copy-done
  390.7 0.0 copy-start.1
  390.7 2.5 convert_element_type.3
  393.2 0.0 copy-done.1
  393.2 1.3 copy.36
  (1 shorter events, 0.0 us)
Async XLA Ops:
  383.3 7.4 %copy-start = (bf16[4,256,1024]{2,1,0:T(8,128)(2,1)S(1)}, bf16[4,256,1024]{2,1,0:T(8,128)(2,1)}, u32[]{:S(2)}) copy-start(bf16[4,256,1024]{2,1,0:T(8,128)(2,1)} %get-tuple-element.23) | copy-start | bytes 6291460
  390.7 2.5 copy-start.1

commit v3 on v2

--- a/solution.py
+++ b/solution.py
@@ -99,10 +99,14 @@
     xg_u,
     xg_q,
     xg_o,
-    zg_d,
-    zg_u,
-    zg_q,
-    zg_o,
+    zf_d,
+    zf_u,
+    zf_q,
+    zf_o,
+    zp_d,
+    zp_u,
+    zp_q,
+    zp_o,
     sums,
     sm,
     smz,
@@ -127,8 +131,12 @@
     out_r,
     gx_s,
     gx_r,
+    gy_s,
+    gy_r,
     gz_s,
     gz_r,
+    line_s,
+    line_r,
     sm_s,
     sm_r,
 ):
@@ -181,56 +189,90 @@
     def own_rows(cc):
         return aligned(f * nc + cc, rows_w)
 
-    def w_start(g):
+    def own_copies(g):
         srcs, stage, _ = groups[g]
         for k, src in enumerate(srcs):
             cols = pl.ds(k * src.shape[1], src.shape[1])
-            pltpu.make_async_copy(src, stage.at[t, :, cols], wz_r.at[g, 0]).start()
+            dst = stage.at[t, :, cols]
+            pltpu.make_async_copy(src, dst, wz_r.at[g, 0]).start()
+            yield src, dst
+
+    def w_start(g):
+        for src, dst in own_copies(g):
             for j in range(1, nt):
-                remote(
-                    src,
-                    stage.at[t, :, cols],
-                    wz_s.at[g, j],
-                    wz_r.at[g, j],
-                    (f, c, lax.rem(t + j, nt)),
-                ).start()
+                remote(src, dst, wz_s.at[g, j], wz_r.at[g, j], (f, c, lax.rem(t + j, nt))).start()
+
+    def w_cross_block(g, ts):
+        _, stage, final = groups[g]
+
+        @pl.when(ts == c)
+        def _():
+            pltpu.make_async_copy(stage.at[ts], final.at[own_rows(c)], wy_r.at[g, c]).start()
+
+        @pl.when(ts != c)
+        def _():
+            remote(
+                stage.at[ts], final.at[own_rows(c)], wy_s.at[g, ts], wy_r.at[g, c], (f, ts, t)
+            ).start()
 
     def w_cross(g, j):
-        _, stage, final = groups[g]
+        stage = groups[g][1]
         ts = lax.rem(t + nt - j, nt)
         if j == 0:
             pltpu.make_async_copy(stage.at[ts], stage.at[ts], wz_r.at[g, 0]).wait()
         else:
             remote(stage.at[ts], stage.at[ts], wz_s.at[g, j], wz_r.at[g, j], (f, c, ts)).wait_recv()
-
-        @pl.when(ts == c)
+        w_cross_block(g, ts)
+
+    def hops(send, h):
+        @pl.when((t >= h) & (t < nt - 1))
         def _():
-            pltpu.make_async_copy(stage.at[ts], final.at[own_rows(c)], wy_r.at[g, c]).start()
-
-        @pl.when(ts != c)
+            send(t - h, h + 1, t + 1)
+
+        @pl.when((t + h < nt) & (t > 0))
         def _():
-            remote(
-                stage.at[ts], final.at[own_rows(c)], wy_s.at[g, j], wy_r.at[g, c], (f, ts, t)
-            ).start()
+            send(t + h, nt + h, t - 1)
+
+    def arrivals(take, h):
+        @pl.when(t >= h)
+        def _():
+            take(t - h, h, t - 1)
+
+        @pl.when(t + h < nt)
+        def _():
+            take(t + h, nt - 1 + h, t + 1)
+
+    def w_line_copy(g, src, ts, n, to):
+        return remote(
+            src, groups[g][1].at[ts], wz_s.at[g, n], wz_r.at[g, n], (f, c, to)
+        )
+
+    def w_line_start(g):
+        for src, _ in own_copies(g):
+            hops(lambda ts, n, to: w_line_copy(g, src, ts, n, to).start(), 0)
+
+    def w_line(g, h):
+        stage = groups[g][1]
+
+        def take(ts, n, source):
+            w_line_copy(g, stage.at[ts], ts, n, source).wait_recv()
+
+        arrivals(take, h)
+        if h < nt - 1:
+            hops(lambda ts, n, to: w_line_copy(g, stage.at[ts], ts, n, to).start(), h)
+        arrivals(lambda ts, n, source: w_cross_block(g, ts), h)
 
     def w_spread(g, i):
         _, _, final = groups[g]
         cc = lax.rem(c + i, nc)
+        part = final.at[own_rows(cc)]
         if i == 0:
-            pltpu.make_async_copy(
-                final.at[own_rows(cc)], final.at[own_rows(cc)], wy_r.at[g, cc]
-            ).wait()
+            pltpu.make_async_copy(part, part, wy_r.at[g, cc]).wait()
         else:
-            remote(
-                final.at[own_rows(cc)], final.at[own_rows(cc)], wy_s.at[g, 0], wy_r.at[g, cc], (f, cc, t)
-            ).wait_recv()
+            remote(part, part, wy_s.at[g, 0], wy_r.at[g, cc], (f, cc, t)).wait_recv()
         for df in range(1, nf):
             remote(
-                final.at[own_rows(cc)],
-                final.at[own_rows(cc)],
-                wx_s.at[g, df],
-                wx_r.at[g, df],
-                (lax.rem(f + df, nf), c, t),
+                part, part, wx_s.at[g, df], wx_r.at[g, df], (lax.rem(f + df, nf), c, t)
             ).start()
 
     def w_wait(g):
@@ -242,17 +284,23 @@
 
     def w_finish(g):
         _, stage, final = groups[g]
-        for j in range(1, nt):
-            remote(
-                stage.at[0], stage.at[0], wz_s.at[g, j], wz_r.at[g, j], (f, c, lax.rem(t + j, nt))
-            ).wait_send()
+        if g < 2:
+            for j in range(1, nt):
+                remote(
+                    stage.at[0], stage.at[0], wz_s.at[g, j], wz_r.at[g, j], (f, c, lax.rem(t + j, nt))
+                ).wait_send()
+        else:
+            for h in range(nt - 1):
+                hops(
+                    lambda ts, n, to: w_line_copy(g, stage.at[ts], ts, n, to).wait_send(), h
+                )
         for j in range(nt):
             ts = lax.rem(t + nt - j, nt)
 
             @pl.when(ts != c)
             def _():
                 remote(
-                    stage.at[ts], final.at[own_rows(c)], wy_s.at[g, j], wy_r.at[g, c], (f, ts, t)
+                    stage.at[ts], final.at[own_rows(c)], wy_s.at[g, ts], wy_r.at[g, c], (f, ts, t)
                 ).wait_send()
 
         for df in range(1, nf):
@@ -365,14 +413,17 @@
     pltpu.make_async_copy(x_h.at[t], x_tok.at[aligned(c, seq)], loc_sem.at[0]).wait()
     for k in range(CHUNKS):
         ag_send(x_tok, 0, k)
-    w_cross(0, 0)
+    w_start(1)
+    w_line_start(2)
+    for _ in own_copies(3):
+        pass
+    for g in range(4):
+        w_cross(g, 0)
     sums[...] = jnp.zeros_like(sums)
     for k in range(CHUNKS):
         ag_pass(x_tok, 0, k)
     for j in range(1, nt):
         w_cross(0, j)
-    for g in range(1, 4):
-        w_start(g)
 
     @pl.when(t == c)
     def _():
@@ -384,11 +435,13 @@
 
     for i in range(nc):
         w_spread(0, i)
+    for j in range(1, nt):
+        w_cross(1, j)
     for k in range(CHUNKS):
         ag_wait(x_tok, 0, k, 0)
         ag_wait(x_tok, 0, k, 2)
-    for g in range(1, 4):
-        w_cross(g, 0)
+    for i in range(nc):
+        w_spread(1, i)
     w_wait(0)
 
     def project(b, _):
@@ -438,23 +491,25 @@
         ab = att[aligned(b, seq)]
         return lambda n: dot_last(ab, wo[aligned(n, TILE)])
 
+    w_line(2, 1)
+    for g in (3,):
+        for k, src in enumerate(groups[g][0]):
+            hops(lambda ts, n, to: w_line_copy(g, src, ts, n, to).start(), 0)
     attend(c_ysib)
-    for j in range(1, nt):
-        w_cross(1, j)
     attend(c_y)
-    for i in range(nc):
-        w_spread(1, i)
+    w_line(2, 2)
     w_wait(1)
     rs_sib(0, 0, out_proj(c_ysib))
     rs_y(0, out_proj(c_y))
-    for j in range(1, nt):
-        w_cross(2, j)
     attend(c_sib)
     rs_sib(0, 1, out_proj(c_sib))
+    w_line(2, 3)
+    w_line(3, 1)
     for i in range(nc):
         w_spread(2, i)
     attend(c)
     rs_own(0, out_proj(c))
+    w_line(3, 2)
     rs_copy(0, 1).wait_recv()
 
     b_out, gain1, shift1 = vec[0:1], vec[1:2], vec[2:3]
@@ -476,8 +531,9 @@
     for k in range(CHUNKS):
         rs_rows(0, k, norm1)
         ag_send(nl, 1, k)
-    for j in range(1, nt):
-        w_cross(3, j)
+    w_line(3, 3)
+    for i in range(nc):
+        w_spread(3, i)
     w_wait(2)
 
     def up(b):
@@ -500,8 +556,6 @@
         return lambda n: dot_last(ab, wd[aligned(n, TILE)])
 
     up(c)
-    for i in range(nc):
-        w_spread(3, i)
     for k in range(CHUNKS):
         ag_wait(nl, 1, k, 0)
     up(c_sib)
@@ -517,6 +571,8 @@
     rs_sib(1, 0, down(c_ysib))
     rs_y(1, down(c_y))
     rs_copy(1, 1).wait_recv()
+    for g in range(4):
+        w_finish(g)
     pltpu.make_async_copy(ct_h.at[t], ct_s, loc_sem.at[1]).wait()
 
     def norm2(rows, i):
@@ -583,79 +639,125 @@
 
         lax.fori_loop(0, width // TILE, step, 0)
 
-    grads = ((gwd, xg_d, zg_d), (gwu, xg_u, zg_u), (gwo, xg_o, zg_o), (gqkv, xg_q, zg_q))
-    part_rows = nc * rows_w
-
-    def gx_copy(g, df, dev_f):
-        buf, got, _ = grads[g]
+    grads = (
+        (gwd, xg_d, z3, zf_d, zp_d),
+        (gwu, xg_u, z2, zf_u, zp_u),
+        (gwo, xg_o, z1, zf_o, zp_o),
+        (gqkv, xg_q, z0, zf_q, zp_q),
+    )
+    pair = t + 1 - 2 * lax.rem(t, 2)
+    inner = (t == 1) | (t == nt - 2)
+    far_in = jnp.where(t < 2, 2, 1)
+    far_out = jnp.where(t < 2, nt - 1, 0)
+
+    def gx_copy(g, df, i, dev_f):
+        buf, got = grads[g][:2]
+        cc = lax.rem(c + i, nc)
         return remote(
-            buf.at[aligned(dev_f, part_rows)],
-            got.at[df - 1],
-            gx_s.at[g, df],
-            gx_r.at[g, df],
+            buf.at[aligned(dev_f * nc + cc, rows_w)],
+            got.at[df - 1, aligned(cc, rows_w)],
+            gx_s.at[g, df, i],
+            gx_r.at[g, df, i],
             (dev_f, c, t),
         )
 
+    order = tuple(range(1, nc)) + (0,)
+
     def g_start(g):
+        for i in order:
+            for df in range(1, nf):
+                gx_copy(g, df, i, lax.rem(f + df, nf)).start()
+
+    def gy_copy(g, i, slot, cc):
+        buf, _, got = grads[g][:3]
+        return remote(
+            buf.at[own_rows(cc)], got.at[slot], gy_s.at[g, i], gy_r.at[g, i], (f, cc, t)
+        )
+
+    def g_cross(g, i):
+        buf, got, held = grads[g][:3]
+        cc = lax.rem(c + i, nc)
         for df in range(1, nf):
-            gx_copy(g, df, lax.rem(f + df, nf)).start()
-
-    def gz_copy(g, dc):
-        buf, _, got = grads[g]
-        cc = lax.rem(c + dc, nc)
-        return remote(buf.at[own_rows(cc)], got.at[t], gz_s.at[g, dc], gz_r.at[g, t], (f, cc, c))
-
-    def g_cross(g):
-        buf, got, _ = grads[g]
-        for df in range(1, nf):
-            gx_copy(g, df, lax.rem(f + nf - df, nf)).wait_recv()
-
-        def add(i, _):
-            rows = pl.ds(pl.multiple_of(f * part_rows + i * ROWS, ROWS), ROWS)
+            gx_copy(g, df, i, lax.rem(f + nf - df, nf)).wait_recv()
+
+        def add(n, _):
+            rows = pl.ds(pl.multiple_of((f * nc + cc) * rows_w + n * ROWS, ROWS), ROWS)
             total = buf[rows].astype(F32)
             for df in range(1, nf):
-                total = total + got[df - 1, pl.ds(pl.multiple_of(i * ROWS, ROWS), ROWS)].astype(F32)
-            buf[rows] = total.astype(BF16)
+                theirs = pl.ds(pl.multiple_of(cc * rows_w + n * ROWS, ROWS), ROWS)
+                total = total + got[df - 1, theirs].astype(F32)
+            if i:
+                buf[rows] = total.astype(BF16)
+            else:
+                held[c, pl.ds(pl.multiple_of(n * ROWS, ROWS), ROWS)] = total.astype(BF16)
             return 0
 
-        lax.fori_loop(0, part_rows // ROWS, add, 0)
-        for dc in range(1, nc):
-            gz_copy(g, dc).start()
-
-        @pl.when(t != c)
+        lax.fori_loop(0, rows_w // ROWS, add, 0)
+        if i:
+            gy_copy(g, i, c, cc).start()
+
+    def gz_copy(g, n, src, dst, to):
+        return remote(src, dst, gz_s.at[g, n], gz_r.at[g, n], (f, c, to))
+
+    def g_line(g):
+        _, _, held, final, part = grads[g]
+        for i in range(1, nc):
+            cs = lax.rem(c + nc - i, nc)
+            gy_copy(g, i, cs, cs).wait_recv()
+
+        @pl.when(jnp.logical_not(inner))
         def _():
-            gz_copy(g, 0).start()
-
-        @pl.when(t == c)
+            gz_copy(g, 2, held.at[far_out], part.at[1], pair).start()
+            gz_copy(g, 1, held.at[far_in], part.at[0], pair).start()
+
+        gz_copy(g, 0, held.at[pair], final.at[0], pair).start()
+
+    def g_relay(g):
+        _, _, held, final, part = grads[g]
+
+        @pl.when(inner)
         def _():
-            pltpu.make_async_copy(
-                buf.at[own_rows(c)], grads[g][2].at[t], gz_r.at[g, t]
-            ).start()
+            for n, (to, slot) in enumerate(((far_out, 1), (far_in, 0))):
+                gz_copy(g, 1 + slot, held.at[to], part.at[slot], pair).wait_recv()
+
+                def add(m, _):
+                    rows = pl.ds(pl.multiple_of(m * ROWS, ROWS), ROWS)
+                    held[to, rows] = (
+                        held[to, rows].astype(F32) + part[slot, rows].astype(F32)
+                    ).astype(BF16)
+                    return 0
+
+                lax.fori_loop(0, rows_w // ROWS, add, 0)
+                remote(
+                    held.at[to], final.at[1], gz_s.at[g, 1 + slot], gz_r.at[g, 3], (f, c, to)
+                ).start()
 
     def g_out(g, store):
-        _, _, got = grads[g]
-        for s in range(nt):
-            remote(got.at[s], got.at[s], gz_s.at[g, 0], gz_r.at[g, s], (f, t, s)).wait_recv()
-
-        def add(i, _):
-            rows = pl.ds(pl.multiple_of(i * ROWS, ROWS), ROWS)
-            total = got[0, rows].astype(F32)
-            for s in range(1, nt):
-                total = total + got[s, rows].astype(F32)
-            store(rows, total)
+        _, _, held, final, _ = grads[g]
+        gz_copy(g, 0, held.at[t], final.at[0], pair).wait_recv()
+        gz_copy(g, 3, held.at[t], final.at[1], far_in).wait_recv()
+
+        def add(m, _):
+            rows = pl.ds(pl.multiple_of(m * ROWS, ROWS), ROWS)
+            store(
+                rows,
+                held[t, rows].astype(F32)
+                + final[0, rows].astype(F32)
+                + final[1, rows].astype(F32),
+            )
             return 0
 
         lax.fori_loop(0, rows_w // ROWS, add, 0)
 
     def g_finish(g):
-        for df in range(1, nf):
-            gx_copy(g, df, lax.rem(f + df, nf)).wait_send()
-        for dc in range(1, nc):
-            gz_copy(g, dc).wait_send()
-
-        @pl.when(t != c)
-        def _():
-            gz_copy(g, 0).wait_send()
+        _, _, held, final, part = grads[g]
+        for i in order:
+            for df in range(1, nf):
+                gx_copy(g, df, i, lax.rem(f + df, nf)).wait_send()
+        for i in range(1, nc):
+            gy_copy(g, i, c, lax.rem(c + i, nc)).wait_send()
+        for n in range(3):
+            gz_copy(g, n, held.at[0], final.at[0], pair).wait_send()
 
     back(c)
     for k in range(CHUNKS):
@@ -673,6 +775,8 @@
     rs_y(2, up_back(c_y))
     weight_grad(gwd, dl2, act)
     g_start(0)
+    weight_grad(gwu, nl, dpl)
+    g_start(1)
     rs_copy(2, 1).wait_recv()
 
     def norm1_back(rows, i):
@@ -689,8 +793,6 @@
     for k in range(CHUNKS):
         rs_rows(2, k, norm1_back)
         ag_send(dl1, 3, k)
-    weight_grad(gwu, nl, dpl)
-    g_start(1)
 
     dk_acc[...] = jnp.zeros_like(dk_acc)
     dv_acc[...] = jnp.zeros_like(dv_acc)
@@ -721,19 +823,26 @@
         sums[7, :, 0:hid] = sums[7, :, 0:hid] + jnp.sum(dqf.reshape(seq // 8, 8, hid), 0)
 
     attend_back(c)
+    g_cross(0, 1)
+    g_cross(0, 2)
     for k in range(CHUNKS):
         ag_wait(dl1, 3, k, 0)
     for k in range(CHUNKS):
         ag_pass(dl1, 3, k)
     attend_back(c_sib)
-    g_cross(0)
+    g_cross(0, 3)
+    g_cross(0, 0)
     attend_back(c_y)
     for k in range(CHUNKS):
         ag_wait(dl1, 3, k, 2)
     weight_grad(gwo, dl1, att)
     g_start(2)
+    g_line(0)
+    for i in order:
+        g_cross(1, i)
     attend_back(c_ysib)
-    g_cross(1)
+    g_relay(0)
+    g_line(1)
 
     def finish_kv(b, _):
         rows = aligned(b, seq)
@@ -764,15 +873,40 @@
 
     for j in range(1, nt):
         sm_copy(0, j, sm, smz.at[j], (f, c, lax.rem(t + j, nt))).start()
+    for i in order:
+        g_cross(2, i)
+    g_relay(1)
     rs_copy(3, 1).wait_recv()
 
     def grad_in(rows, i):
         gi_s[rows] = (dres[rows] + rs_row(rows)).astype(BF16)
 
+    def line_copy(k, src, ts, n, to):
+        rows = pl.ds(k * chunk, chunk)
+        return remote(
+            src.at[rows], gi_h.at[ts, rows], line_s.at[k, n], line_r.at[k, n], (f, c, to)
+        )
+
     for k in range(CHUNKS):
         rs_rows(3, k, grad_in)
-    spread(gi_s, gi_h, 1)
-    g_cross(2)
+        rows = pl.ds(k * chunk, chunk)
+        pltpu.make_async_copy(gi_s.at[rows], gi_h.at[t, rows], line_r.at[k, 0]).start()
+        hops(lambda ts, n, to: line_copy(k, gi_s, ts, n, to).start(), 0)
+    g_line(2)
+
+    def line_hop(k, h):
+        arrivals(lambda ts, n, source: line_copy(k, gi_h.at[ts], ts, n, source).wait_recv(), h)
+        if h < nt - 1:
+            hops(lambda ts, n, to: line_copy(k, gi_h.at[ts], ts, n, to).start(), h)
+
+    for i in order[:2]:
+        g_cross(3, i)
+    for k in range(CHUNKS):
+        line_hop(k, 1)
+    for i in order[2:]:
+        g_cross(3, i)
+    g_line(3)
+    g_relay(2)
     total = sm[...]
     for j in range(1, nt):
         sm_copy(0, j, sm, smz.at[j], (f, c, lax.rem(t + nt - j, nt))).wait_recv()
@@ -780,14 +914,8 @@
     smz[0] = total
     for df in range(1, nf):
         sm_copy(1, df, smz.at[0], smx.at[df], (lax.rem(f + df, nf), c, t)).start()
-    g_cross(3)
-
-    def store_at(out, base):
-        def store(rows, value):
-            out[rows, base : base + value.shape[1]] = value
-
-        return store
-
+    for k in range(CHUNKS):
+        line_hop(k, 2)
     for df in range(1, nf):
         sm_copy(1, df, smz.at[0], smx.at[df], (lax.rem(f + nf - df, nf), c, t)).wait_recv()
         total = total + smx[df]
@@ -795,6 +923,14 @@
     for dc in range(1, nc):
         sm_copy(2, dc, smx.at[0], smc.at[c], (f, lax.rem(c + dc, nc), t)).start()
     smc[c] = total
+    g_relay(3)
+
+    def store_at(out, base):
+        def store(rows, value):
+            out[rows, base : base + value.shape[1]] = value
+
+        return store
+
     g_out(0, store_at(gffn_o, ff))
     g_out(1, store_at(gffn_o, 0))
     g_out(2, store_at(gatt_o, 3 * hid))
@@ -808,10 +944,14 @@
     small_o[6:8] = smc[t, 6:8]
     g_out(3, store_at(gatt_o, 0))
     spread_wait(res_s, res_h, 0)
-    spread_wait(gi_s, gi_h, 1)
+    for k in range(CHUNKS):
+        line_hop(k, 3)
+        rows = pl.ds(k * chunk, chunk)
+        pltpu.make_async_copy(gi_s.at[rows], gi_h.at[t, rows], line_r.at[k, 0]).wait()
+        for h in range(nt - 1):
+            hops(lambda ts, n, to: line_copy(k, gi_h.at[ts], ts, n, to).wait_send(), h)
 
     for g in range(4):
-        w_finish(g)
         g_finish(g)
     for a, buf in enumerate((x_tok, nl, dl2, dl1)):
         ag_finish(buf, a)
@@ -939,10 +1079,14 @@
             vb(nf - 1, part, ff),
             vb(nf - 1, part, 3 * hid),
             vb(nf - 1, part, hid),
-            vb(nt, rows_w, ff),
-            vb(nt, rows_w, ff),
-            vb(nt, rows_w, 3 * hid),
-            vb(nt, rows_w, hid),
+            vb(2, rows_w, ff),
+            vb(2, rows_w, ff),
+            vb(2, rows_w, 3 * hid),
+            vb(2, rows_w, hid),
+            vb(2, rows_w, ff),
+            vb(2, rows_w, ff),
+            vb(2, rows_w, 3 * hid),
+            vb(2, rows_w, hid),
             vf(8, 8, width),
             vf(8, width),
             vf(nt, 8, width),
@@ -951,8 +1095,8 @@
             sem(3),
             sem(nt),
             sem(1),
-            sem(4, nt),
-            sem(4, nt),
+            sem(4, 2 * nt),
+            sem(4, 2 * nt),
             sem(4, nt),
             sem(4, nc),
             sem(4, nf),
@@ -963,12 +1107,16 @@
             sem(4, 2),
             sem(4, CHUNKS),
             sem(4, CHUNKS),
-            sem(2, nt),
-            sem(2, nt),
-            sem(4, nf),
-            sem(4, nf),
+            sem(1, nt),
+            sem(1, nt),
+            sem(4, nf, nc),
+            sem(4, nf, nc),
             sem(4, nc),
-            sem(4, nt),
+            sem(4, nc),
+            sem(4, 3),
+            sem(4, 4),
+            sem(CHUNKS, 2 * nt),
+            sem(CHUNKS, 2 * nt),
             sem(3, max(nf, nc)),
             sem(3, max(nf, nc)),
         ],

time: 395 us -> 294 us (0.74)
  Pallas kernels: 380 us -> 279 us
    pallas_call x1, Pallas kernels: 380 us -> 279 us  [shards(): pl.pallas_call(functools.partial(layer, dims), out_shape=(jax.ShapeDtypeS...]
where the time goes in v3:
time: 294 us; the launch traced here: 293 us
  Pallas kernels  279 us (95%)
  local copies, waits for them, and re-layouts  10.8 us (4%)
  other arithmetic  3.2 us (1%)
    pallas_call x1, Pallas kernels, shards(): pl.pallas_call(functools.partial(layer, dims), out_shape=(jax.ShapeDtypeS...  279 us

profile of v3, /device:TPU:0, one launch (start us, length us, event | category | flops | bytes accessed | tf_op | source)
XLA Modules:
  0.0 293.2 jit_solution(12291913585999173692)
XLA Ops:
  0.7 0.7 pad_maximum_fusion
  1.4 1.4 stack.31.vec
  2.8 0.6 broadcast_in_dim.2.bias_h
  3.4 278.6 %shard_map.305 = (bf16[4,256,1024]{2,1,0:T(8,128)(2,1)}, bf16[4,256,1024]{2,1,0:T(8,128)(2,1)}, f32[128,2048]{1,0:T(8,128)}, f32[128,1024]{1,0:T(8,128)}, f32[8,1024]{1,0:T(8,128)}) custom-call(s32[4]{0:T(128)} %lens.1, bf16[4,256,1024]{2,1,0:T(8,128)(2,1)} %x_h.1, bf16[4,256,1024]{2,1,0:T(8,128)(2,1)} %ct_h.1, bf16[128,256]{1,0:T(8,128)(2,1)} %wq_h.1, ...), custom_call_target="tpu_custom_call" | custom-call | tf_op jit(solution)/shard_map/pallas_call | solution.py:1022
  282.0 0.0 copy-start
  282.1 1.4 fusion.3
  283.5 1.8 fusion.2
  285.3 1.9 fusion.1
  287.1 2.3 fusion
  289.4 0.0 copy-done
  289.4 0.0 copy-start.1
  289.4 2.5 convert_element_type.3
  291.9 0.0 copy-done.1
  291.9 1.3 copy.36
  (1 shorter events, 0.0 us)
Async XLA Ops:
  282.0 7.4 %copy-start = (bf16[4,256,1024]{2,1,0:T(8,128)(2,1)S(1)}, bf16[4,256,1024]{2,1,0:T(8,128)(2,1)}, u32[]{:S(2)}) copy-start(bf16[4,256,1024]{2,1,0:T(8,128)(2,1)} %get-tuple-element.23) | copy-start | bytes 6291460
  289.4 2.5 copy-start.1

commit v4 on v3

--- a/solution.py
+++ b/solution.py
@@ -44,12 +44,23 @@
     wo_h,
     wu_h,
     wd_h,
-    bias_h,
-    vec,
+    bq_h,
+    bv_h,
+    bu_h,
+    b_out_r,
+    gain1_r,
+    shift1_r,
+    b_down_r,
+    gain2_r,
+    shift2_r,
     res_h,
     gi_h,
-    gffn_o,
-    gatt_o,
+    gq_o,
+    gk_o,
+    gv_o,
+    go_o,
+    gu_o,
+    gd_o,
     small_o,
     wqkv,
     wo,
@@ -189,17 +200,37 @@
     def own_rows(cc):
         return aligned(f * nc + cc, rows_w)
 
-    def own_copies(g):
+    def hops(send, h):
+        @pl.when((t >= h) & (t < nt - 1))
+        def _():
+            send(t - h, h + 1, t + 1)
+
+        @pl.when((t + h < nt) & (t > 0))
+        def _():
+            send(t + h, nt + h, t - 1)
+
+    def arrivals(take, h):
+        @pl.when(t >= h)
+        def _():
+            take(t - h, h, t - 1)
+
+        @pl.when(t + h < nt)
+        def _():
+            take(t + h, nt - 1 + h, t + 1)
+
+    def w_line_copy(g, src, ts, n, to):
+        return remote(
+            src, groups[g][1].at[ts], wz_s.at[g, n], wz_r.at[g, n], (f, c, to)
+        )
+
+    def w_start(g):
         srcs, stage, _ = groups[g]
         for k, src in enumerate(srcs):
-            cols = pl.ds(k * src.shape[1], src.shape[1])
-            dst = stage.at[t, :, cols]
+            dst = stage.at[t, :, pl.ds(k * src.shape[1], src.shape[1])]
             pltpu.make_async_copy(src, dst, wz_r.at[g, 0]).start()
-            yield src, dst
-
-    def w_start(g):
-        for src, dst in own_copies(g):
-            for j in range(1, nt):
+            if g:
+                hops(lambda ts, n, to: w_line_copy(g, src, ts, n, to).start(), 0)
+            for j in range(1, 1 if g else nt):
                 remote(src, dst, wz_s.at[g, j], wz_r.at[g, j], (f, c, lax.rem(t + j, nt))).start()
 
     def w_cross_block(g, ts):
@@ -223,33 +254,6 @@
         else:
             remote(stage.at[ts], stage.at[ts], wz_s.at[g, j], wz_r.at[g, j], (f, c, ts)).wait_recv()
         w_cross_block(g, ts)
-
-    def hops(send, h):
-        @pl.when((t >= h) & (t < nt - 1))
-        def _():
-            send(t - h, h + 1, t + 1)
-
-        @pl.when((t + h < nt) & (t > 0))
-        def _():
-            send(t + h, nt + h, t - 1)
-
-    def arrivals(take, h):
-        @pl.when(t >= h)
-        def _():
-            take(t - h, h, t - 1)
-
-        @pl.when(t + h < nt)
-        def _():
-            take(t + h, nt - 1 + h, t + 1)
-
-    def w_line_copy(g, src, ts, n, to):
-        return remote(
-            src, groups[g][1].at[ts], wz_s.at[g, n], wz_r.at[g, n], (f, c, to)
-        )
-
-    def w_line_start(g):
-        for src, _ in own_copies(g):
-            hops(lambda ts, n, to: w_line_copy(g, src, ts, n, to).start(), 0)
 
     def w_line(g, h):
         stage = groups[g][1]
@@ -284,16 +288,13 @@
 
     def w_finish(g):
         _, stage, final = groups[g]
-        if g < 2:
-            for j in range(1, nt):
-                remote(
-                    stage.at[0], stage.at[0], wz_s.at[g, j], wz_r.at[g, j], (f, c, lax.rem(t + j, nt))
-                ).wait_send()
-        else:
+        if g:
             for h in range(nt - 1):
-                hops(
-                    lambda ts, n, to: w_line_copy(g, stage.at[ts], ts, n, to).wait_send(), h
-                )
+                hops(lambda ts, n, to: w_line_copy(g, stage.at[ts], ts, n, to).wait_send(), h)
+        for j in range(1, 1 if g else nt):
+            remote(
+                stage.at[0], stage.at[0], wz_s.at[g, j], wz_r.at[g, j], (f, c, lax.rem(t + j, nt))
+            ).wait_send()
         for j in range(nt):
             ts = lax.rem(t + nt - j, nt)
 
@@ -404,45 +405,59 @@
     pltpu.make_async_copy(x_h.at[t], x_tok.at[aligned(c, seq)], loc_sem.at[0]).start()
     pltpu.make_async_copy(ct_h.at[t], ct_s, loc_sem.at[1]).start()
 
+    biases = (
+        (bq_h, bias.at[:, pl.ds(0, hid)]),
+        (bv_h, bias.at[:, pl.ds(hid, hid)]),
+        (bu_h, bias.at[:, pl.ds(2 * hid, ff)]),
+    )
+
     @pl.when(t == c)
     def _():
-        pltpu.make_async_copy(bias_h, bias, loc_sem.at[2]).start()
-        for j in range(1, nt):
-            remote(bias_h, bias, bias_s.at[j], bias_r.at[0], (f, c, lax.rem(t + j, nt))).start()
+        for src, dst in biases:
+            pltpu.make_async_copy(src, dst, loc_sem.at[2]).start()
+            for j in range(1, nt):
+                remote(src, dst, bias_s.at[j], bias_r.at[0], (f, c, lax.rem(t + j, nt))).start()
 
     pltpu.make_async_copy(x_h.at[t], x_tok.at[aligned(c, seq)], loc_sem.at[0]).wait()
     for k in range(CHUNKS):
         ag_send(x_tok, 0, k)
     w_start(1)
-    w_line_start(2)
-    for _ in own_copies(3):
-        pass
-    for g in range(4):
-        w_cross(g, 0)
+    w_start(2)
+    w_cross(0, 0)
+    w_cross(1, 0)
     sums[...] = jnp.zeros_like(sums)
-    for k in range(CHUNKS):
+    w_cross(0, 1)
+    ag_pass(x_tok, 0, 0)
+    w_cross(0, 2)
+    for k in range(1, CHUNKS):
         ag_pass(x_tok, 0, k)
-    for j in range(1, nt):
-        w_cross(0, j)
+    w_cross(0, 3)
+    w_cross(2, 0)
+    w_line(1, 1)
+    for i in range(nc):
+        w_spread(0, i)
+    w_start(3)
+    w_line(1, 2)
+    w_line(2, 1)
+    w_cross(3, 0)
+    w_line(1, 3)
+    for i in range(nc):
+        w_spread(1, i)
 
     @pl.when(t == c)
     def _():
-        pltpu.make_async_copy(bias_h, bias, loc_sem.at[2]).wait()
+        pltpu.make_async_copy(bias, bias, loc_sem.at[2]).wait()
 
     @pl.when(t != c)
     def _():
-        remote(bias_h, bias, bias_s.at[0], bias_r.at[0], (f, c, c)).wait_recv()
-
-    for i in range(nc):
-        w_spread(0, i)
-    for j in range(1, nt):
-        w_cross(1, j)
+        remote(bias, bias, bias_s.at[0], bias_r.at[0], (f, c, c)).wait_recv()
+
     for k in range(CHUNKS):
         ag_wait(x_tok, 0, k, 0)
         ag_wait(x_tok, 0, k, 2)
-    for i in range(nc):
-        w_spread(1, i)
     w_wait(0)
+    w_line(3, 1)
+    w_line(2, 2)
 
     def project(b, _):
         rows = aligned(b, seq)
@@ -491,29 +506,26 @@
         ab = att[aligned(b, seq)]
         return lambda n: dot_last(ab, wo[aligned(n, TILE)])
 
-    w_line(2, 1)
-    for g in (3,):
-        for k, src in enumerate(groups[g][0]):
-            hops(lambda ts, n, to: w_line_copy(g, src, ts, n, to).start(), 0)
     attend(c_ysib)
+    w_line(3, 2)
+    w_line(2, 3)
     attend(c_y)
-    w_line(2, 2)
+    for i in range(nc):
+        w_spread(2, i)
     w_wait(1)
     rs_sib(0, 0, out_proj(c_ysib))
+    w_line(3, 3)
     rs_y(0, out_proj(c_y))
+    for i in range(nc):
+        w_spread(3, i)
     attend(c_sib)
     rs_sib(0, 1, out_proj(c_sib))
-    w_line(2, 3)
-    w_line(3, 1)
-    for i in range(nc):
-        w_spread(2, i)
     attend(c)
     rs_own(0, out_proj(c))
-    w_line(3, 2)
     rs_copy(0, 1).wait_recv()
 
-    b_out, gain1, shift1 = vec[0:1], vec[1:2], vec[2:3]
-    b_down, gain2, shift2 = vec[3:4], vec[4:5], vec[5:6]
+    b_out, gain1, shift1 = b_out_r[...], gain1_r[...], shift1_r[...]
+    b_down, gain2, shift2 = b_down_r[...], gain2_r[...], shift2_r[...]
     own = c * seq
 
     def own_slice(rows):
@@ -531,9 +543,6 @@
     for k in range(CHUNKS):
         rs_rows(0, k, norm1)
         ag_send(nl, 1, k)
-    w_line(3, 3)
-    for i in range(nc):
-        w_spread(3, i)
     w_wait(2)
 
     def up(b):
@@ -631,14 +640,6 @@
         pb = dpl[aligned(b, seq)]
         return lambda n: dot_last(pb, wu[aligned(n, TILE)])
 
-    def weight_grad(dst, left, right):
-        def step(m, _):
-            rows = aligned(m, TILE)
-            dst[rows] = dot_first(left[:, rows], right[...]).astype(BF16)
-            return 0
-
-        lax.fori_loop(0, width // TILE, step, 0)
-
     grads = (
         (gwd, xg_d, z3, zf_d, zp_d),
         (gwu, xg_u, z2, zf_u, zp_u),
@@ -663,10 +664,28 @@
 
     order = tuple(range(1, nc)) + (0,)
 
-    def g_start(g):
-        for i in order:
-            for df in range(1, nf):
-                gx_copy(g, df, i, lax.rem(f + df, nf)).start()
+    part_rows = nc * rows_w
+    def weight_grad(g, left, right):
+        dst = grads[g][0]
+
+        def rows_from(first, count):
+            def step(m, _):
+                rows = pl.ds(pl.multiple_of(first + m * TILE, TILE), TILE)
+                dst[rows] = dot_first(left[:, rows], right[...]).astype(BF16)
+                return 0
+
+            lax.fori_loop(0, count // TILE, step, 0)
+
+        split = part_rows % TILE == 0
+        if not split:
+            rows_from(0, width)
+        for df in tuple(range(1, nf)) + (0,):
+            to = lax.rem(f + df, nf)
+            if split:
+                rows_from(to * part_rows, part_rows)
+            if df:
+                for i in order:
+                    gx_copy(g, df, i, to).start()
 
     def gy_copy(g, i, slot, cc):
         buf, _, got = grads[g][:3]
@@ -773,10 +792,8 @@
     back(c_ysib)
     rs_sib(2, 0, up_back(c_ysib))
     rs_y(2, up_back(c_y))
-    weight_grad(gwd, dl2, act)
-    g_start(0)
-    weight_grad(gwu, nl, dpl)
-    g_start(1)
+    weight_grad(0, dl2, act)
+    weight_grad(1, nl, dpl)
     rs_copy(2, 1).wait_recv()
 
     def norm1_back(rows, i):
@@ -827,22 +844,20 @@
     g_cross(0, 2)
     for k in range(CHUNKS):
         ag_wait(dl1, 3, k, 0)
+    attend_back(c_sib)
     for k in range(CHUNKS):
         ag_pass(dl1, 3, k)
-    attend_back(c_sib)
     g_cross(0, 3)
     g_cross(0, 0)
     attend_back(c_y)
+    g_line(0)
     for k in range(CHUNKS):
         ag_wait(dl1, 3, k, 2)
-    weight_grad(gwo, dl1, att)
-    g_start(2)
-    g_line(0)
-    for i in order:
-        g_cross(1, i)
+    weight_grad(2, dl1, att)
+    g_cross(1, 1)
+    g_cross(1, 2)
     attend_back(c_ysib)
     g_relay(0)
-    g_line(1)
 
     def finish_kv(b, _):
         rows = aligned(b, seq)
@@ -864,8 +879,10 @@
     rs_y(3, in_back(c_y))
     rs_sib(3, 1, in_back(c_sib))
     rs_own(3, in_back(c))
-    weight_grad(gqkv, x_tok, dqkv)
-    g_start(3)
+    weight_grad(3, x_tok, dqkv)
+    g_cross(1, 3)
+    g_cross(1, 0)
+    g_line(1)
     sm[...] = jnp.sum(sums[...], 1)
 
     def sm_copy(stage, j, src, dst, dev):
@@ -925,15 +942,16 @@
     smc[c] = total
     g_relay(3)
 
-    def store_at(out, base):
+    def store_in(*outs):
         def store(rows, value):
-            out[rows, base : base + value.shape[1]] = value
+            for k, out in enumerate(outs):
+                out[rows] = value[:, k * out.shape[1] : (k + 1) * out.shape[1]]
 
         return store
 
-    g_out(0, store_at(gffn_o, ff))
-    g_out(1, store_at(gffn_o, 0))
-    g_out(2, store_at(gatt_o, 3 * hid))
+    g_out(0, store_in(gd_o))
+    g_out(1, store_in(gu_o))
+    g_out(2, store_in(go_o))
     for dc in range(1, nc):
         cs = lax.rem(c + nc - dc, nc)
         sm_copy(2, dc, smx.at[0], smc.at[cs], (f, cs, t)).wait_recv()
@@ -942,7 +960,7 @@
         whole = whole + smc[s]
     small_o[0:6] = whole[0:6]
     small_o[6:8] = smc[t, 6:8]
-    g_out(3, store_at(gatt_o, 0))
+    g_out(3, store_in(gq_o, gk_o, gv_o))
     spread_wait(res_s, res_h, 0)
     for k in range(CHUNKS):
         line_hop(k, 3)
@@ -970,8 +988,21 @@
     def _():
         for j in range(1, nt):
             remote(
-                bias_h, bias, bias_s.at[j], bias_r.at[0], (f, c, lax.rem(t + j, nt))
+                bias, bias, bias_s.at[j], bias_r.at[0], (f, c, lax.rem(t + j, nt))
             ).wait_send()
+
+
+def hand_over(small_rows, *refs):
+    whole, small = refs[:8], refs[8]
+    outs, small_o = refs[9:17], refs[17:26]
+
+    @pl.when(pl.program_id(0) == 0)
+    def _():
+        for out, (row, start, size) in zip(small_o, small_rows):
+            out[...] = small[row : row + 1, start : start + size]
+
+    for out, value in zip(outs, whole):
+        out[...] = value[...].astype(out.dtype)
 
 
 def shards(
@@ -1003,9 +1034,20 @@
     tok = seq * nc
     heads = hid // DH
     part = nc * rows_w
-    bias = jnp.broadcast_to(jnp.concatenate([b_query, b_value, b_up])[None], (8, 2 * hid + ff))
-    zero = jnp.zeros_like(b_out)
-    vec = jnp.stack([b_out, gain_attn, shift_attn, b_down, gain_ffn, shift_ffn, zero, zero])
+    rows = [
+        v.reshape(1, -1)
+        for v in (
+            b_query,
+            b_value,
+            b_up,
+            b_out,
+            gain_attn,
+            shift_attn,
+            b_down,
+            gain_ffn,
+            shift_ffn,
+        )
+    ]
     hbm = pl.BlockSpec(memory_space=pl.ANY)
     vmem = pl.BlockSpec(memory_space=pltpu.VMEM)
     smem = pl.BlockSpec(memory_space=pltpu.SMEM)
@@ -1019,17 +1061,17 @@
     def sem(*shape):
         return pltpu.SemaphoreType.DMA(shape)
 
-    result, grad_in, g_ffn, g_att, small = pl.pallas_call(
+    result, grad_in, g_q, g_k, g_v, g_o, g_u, g_d, small = pl.pallas_call(
         functools.partial(layer, dims),
         out_shape=(
             jax.ShapeDtypeStruct((nt, seq, width), BF16),
             jax.ShapeDtypeStruct((nt, seq, width), BF16),
-            jax.ShapeDtypeStruct((rows_w, 2 * ff), F32),
-            jax.ShapeDtypeStruct((rows_w, 4 * hid), F32),
+            *[jax.ShapeDtypeStruct((rows_w, hid), F32)] * 4,
+            *[jax.ShapeDtypeStruct((rows_w, ff), F32)] * 2,
             jax.ShapeDtypeStruct((8, width), F32),
         ),
-        in_specs=[smem] + [hbm] * 9 + [vmem],
-        out_specs=(hbm, hbm, vmem, vmem, vmem),
+        in_specs=[smem] + [hbm] * 11 + [vmem] * 6,
+        out_specs=(hbm, hbm) + (vmem,) * 7,
         scratch_shapes=[
             vb(width, 3 * hid),
             vb(width, hid),
@@ -1070,7 +1112,7 @@
             vb(seq, width),
             vb(seq, width),
             vb(seq, width),
-            vf(8, 2 * hid + ff),
+            vf(1, 2 * hid + ff),
             vb(width, ff),
             vb(width, ff),
             vb(width, 3 * hid),
@@ -1123,25 +1165,46 @@
         compiler_params=pltpu.CompilerParams(
             collective_id=0, has_side_effects=True, vmem_limit_bytes=63 << 20
         ),
-    )(lengths, inputs, cotangent, w_query, w_key, w_value, w_out, w_up, w_down, bias, vec)
+    )(lengths, inputs, cotangent, w_query, w_key, w_value, w_out, w_up, w_down, *rows)
+    small_rows = ((7, 0, hid), (7, hid, hid), (0, 0, width), (1, 0, width), (2, 0, width))
+    small_rows += ((6, 0, ff), (3, 0, width), (4, 0, width), (5, 0, width))
+    whole = (result, g_q, g_k, g_v, g_o, g_u, g_d, grad_in)
+    step = rows_w // nt if rows_w % (8 * nt) == 0 else rows_w
+
+    def block(a):
+        if a.ndim == 3:
+            return pl.BlockSpec((1, seq, width), lambda i: (i, 0, 0))
+        return pl.BlockSpec((step, a.shape[1]), lambda i: (i if step < rows_w else 0, 0))
+
+    outs = pl.pallas_call(
+        functools.partial(hand_over, small_rows),
+        grid=(nt,),
+        out_shape=tuple(jax.ShapeDtypeStruct(a.shape, a.dtype) for a in whole[:7])
+        + (jax.ShapeDtypeStruct(grad_in.shape, F32),)
+        + tuple(jax.ShapeDtypeStruct((1, n), F32) for _, _, n in small_rows),
+        in_specs=[block(a) for a in whole] + [vmem],
+        out_specs=tuple(block(a) for a in whole) + (vmem,) * 9,
+    )(*whole, small)
+    result, g_q, g_k, g_v, g_o, g_u, g_d, grad_in = outs[:8]
+    s_bq, s_bv, s_bo, s_ga, s_sa, s_bu, s_bd, s_gf, s_sf = (a.reshape(-1) for a in outs[8:])
     return (
         result,
-        grad_in.astype(F32),
-        g_att[:, :hid],
-        g_att[:, hid : 2 * hid],
-        g_att[:, 2 * hid : 3 * hid],
-        small[7, :hid],
-        small[7, hid : 2 * hid],
-        g_att[:, 3 * hid :],
-        small[0],
-        small[1],
-        small[2],
-        g_ffn[:, :ff],
-        small[6, :ff],
-        g_ffn[:, ff:],
-        small[3],
-        small[4],
-        small[5],
+        grad_in,
+        g_q,
+        g_k,
+        g_v,
+        s_bq,
+        s_bv,
+        g_o,
+        s_bo,
+        s_ga,
+        s_sa,
+        g_u,
+        s_bu,
+        g_d,
+        s_bd,
+        s_gf,
+        s_sf,
     )
 
 

time: 294 us -> 277 us (0.942)
  local copies, waits for them, and re-layouts: 10.8 us -> 0 us
  Pallas kernels: 279 us -> 275 us
  other arithmetic: 3.2 us -> 0 us
    pallas_call x1, Pallas kernels: 279 us -> 269 us  [shards(): pl.pallas_call(functools.partial(layer, dims), out_shape=(jax.ShapeDtypeS...]
    slice x4 -> x0, local copies, waits for them, and re-layouts: 7.37 us -> none  [the longest x1 2.28 us: shards(): g_ffn[:, ff:]]
    pallas_call x0 -> x1, Pallas kernels: none -> 6.2 us  [shards(): pl.pallas_call(functools.partial(hand_over, small_rows), grid=(nt,), out_...]
where the time goes in v4:
time: 277 us; the launch traced here: 276 us
  Pallas kernels  275 us (99%)
    pallas_call x1, Pallas kernels, shards(): pl.pallas_call(functools.partial(layer, dims), out_shape=(jax.ShapeDtypeS...  269 us
    pallas_call x1, Pallas kernels, shards(): pl.pallas_call(functools.partial(hand_over, small_rows), grid=(nt,), out_...  6.2 us

profile of v4, /device:TPU:0, one launch (start us, length us, event | category | flops | bytes accessed | tf_op | source)
XLA Modules:
  0.0 275.8 jit_solution(13791898264972277011)
XLA Ops:
  0.7 268.8 %shard_map.305 = (bf16[4,256,1024]{2,1,0:T(8,128)(2,1)}, bf16[4,256,1024]{2,1,0:T(8,128)(2,1)}, f32[128,256]{1,0:T(8,128)}, f32[128,256]{1,0:T(8,128)}, f32[128,...) custom-call(s32[4]{0:T(128)} %lens.1, ...), custom_call_target="tpu_custom_call" | custom-call | tf_op jit(solution)/shard_map/pallas_call | solution.py:1064
  269.5 6.2 %shard_map.306 = (bf16[4,256,1024]{2,1,0:T(8,128)(2,1)}, f32[128,256]{1,0:T(8,128)}, f32[128,256]{1,0:T(8,128)}, f32[128,256]{1,0:T(8,128)}, f32[128,256]{1,0:T(...) custom-call(bf16[4,256,1024]{2,1,0:T(8,128)(2,1)} %get-tuple-element, ...), custom_call_target="tpu_custom_call" | custom-call | tf_op jit(solution)/shard_map/pallas_call | solution.py:1179

commit v5 on v4

--- a/solution.py
+++ b/solution.py
@@ -218,6 +218,10 @@
         def _():
             take(t + h, nt - 1 + h, t + 1)
 
+    def w_cross_at(g, h):
+        pl.when(t >= h)(lambda: w_cross(g, h))
+        pl.when(t + h < nt)(lambda: w_cross(g, nt - h))
+
     def w_line_copy(g, src, ts, n, to):
         return remote(
             src, groups[g][1].at[ts], wz_s.at[g, n], wz_r.at[g, n], (f, c, to)
@@ -279,6 +283,12 @@
                 part, part, wx_s.at[g, df], wx_r.at[g, df], (lax.rem(f + df, nf), c, t)
             ).start()
 
+    def w_spread_at(g, h):
+        @pl.when((t - c == h) | (c - t == h))
+        def _():
+            for i in range(nc):
+                w_spread(g, i)
+
     def w_wait(g):
         _, _, final = groups[g]
         for df in range(1, nf):
@@ -426,23 +436,27 @@
     w_cross(0, 0)
     w_cross(1, 0)
     sums[...] = jnp.zeros_like(sums)
-    w_cross(0, 1)
+    w_cross_at(0, 1)
     ag_pass(x_tok, 0, 0)
-    w_cross(0, 2)
+    w_spread_at(0, 0)
+    w_cross_at(0, 2)
     for k in range(1, CHUNKS):
         ag_pass(x_tok, 0, k)
-    w_cross(0, 3)
+    w_spread_at(0, 1)
+    w_cross_at(0, 3)
+    w_spread_at(1, 0)
     w_cross(2, 0)
     w_line(1, 1)
-    for i in range(nc):
-        w_spread(0, i)
+    w_spread_at(0, 2)
     w_start(3)
     w_line(1, 2)
+    w_spread_at(1, 1)
     w_line(2, 1)
+    w_spread_at(0, 3)
+    w_spread_at(2, 0)
     w_cross(3, 0)
     w_line(1, 3)
-    for i in range(nc):
-        w_spread(1, i)
+    w_spread_at(1, 2)
 
     @pl.when(t == c)
     def _():
@@ -457,7 +471,7 @@
         ag_wait(x_tok, 0, k, 2)
     w_wait(0)
     w_line(3, 1)
-    w_line(2, 2)
+    w_spread_at(1, 3)
 
     def project(b, _):
         rows = aligned(b, seq)
@@ -506,20 +520,24 @@
         ab = att[aligned(b, seq)]
         return lambda n: dot_last(ab, wo[aligned(n, TILE)])
 
+    w_line(2, 2)
+    w_spread_at(2, 1)
+    w_spread_at(3, 0)
     attend(c_ysib)
     w_line(3, 2)
+    w_spread_at(2, 2)
+    w_spread_at(3, 1)
+    attend(c_y)
     w_line(2, 3)
-    attend(c_y)
-    for i in range(nc):
-        w_spread(2, i)
     w_wait(1)
     rs_sib(0, 0, out_proj(c_ysib))
+    rs_y(0, out_proj(c_y))
+    w_spread_at(2, 3)
+    w_spread_at(3, 2)
     w_line(3, 3)
-    rs_y(0, out_proj(c_y))
-    for i in range(nc):
-        w_spread(3, i)
     attend(c_sib)
     rs_sib(0, 1, out_proj(c_sib))
+    w_spread_at(3, 3)
     attend(c)
     rs_own(0, out_proj(c))
     rs_copy(0, 1).wait_recv()
@@ -570,15 +588,15 @@
     up(c_sib)
     for k in range(CHUNKS):
         ag_pass(nl, 1, k)
+    up(c_y)
+    for k in range(CHUNKS):
+        ag_wait(nl, 1, k, 2)
+    up(c_ysib)
     w_wait(3)
+    rs_sib(1, 0, down(c_ysib))
+    rs_y(1, down(c_y))
     rs_sib(1, 1, down(c_sib))
     rs_own(1, down(c))
-    up(c_y)
-    for k in range(CHUNKS):
-        ag_wait(nl, 1, k, 2)
-    up(c_ysib)
-    rs_sib(1, 0, down(c_ysib))
-    rs_y(1, down(c_y))
     rs_copy(1, 1).wait_recv()
     for g in range(4):
         w_finish(g)
@@ -858,6 +876,8 @@
     g_cross(1, 2)
     attend_back(c_ysib)
     g_relay(0)
+    g_cross(1, 3)
+    g_cross(1, 0)
 
     def finish_kv(b, _):
         rows = aligned(b, seq)
@@ -877,12 +897,11 @@
 
     rs_sib(3, 0, in_back(c_ysib))
     rs_y(3, in_back(c_y))
+    g_line(1)
     rs_sib(3, 1, in_back(c_sib))
     rs_own(3, in_back(c))
     weight_grad(3, x_tok, dqkv)
-    g_cross(1, 3)
-    g_cross(1, 0)
-    g_line(1)
+    g_relay(1)
     sm[...] = jnp.sum(sums[...], 1)
 
     def sm_copy(stage, j, src, dst, dev):
@@ -892,7 +911,6 @@
         sm_copy(0, j, sm, smz.at[j], (f, c, lax.rem(t + j, nt))).start()
     for i in order:
         g_cross(2, i)
-    g_relay(1)
     rs_copy(3, 1).wait_recv()
 
     def grad_in(rows, i):

time: 277 us -> 262 us (0.946)
  Pallas kernels: 275 us -> 260 us
    pallas_call x1, Pallas kernels: 269 us -> 254 us  [shards(): pl.pallas_call(functools.partial(layer, dims), out_shape=(jax.ShapeDtypeS...]
where the time goes in v5:
time: 262 us; the launch traced here: 261 us
  Pallas kernels  260 us (99%)
    pallas_call x1, Pallas kernels, shards(): pl.pallas_call(functools.partial(layer, dims), out_shape=(jax.ShapeDtypeS...  254 us
    pallas_call x1, Pallas kernels, shards(): pl.pallas_call(functools.partial(hand_over, small_rows), grid=(nt,), out_...  6.2 us

profile of v5, /device:TPU:0, one launch (start us, length us, event | category | flops | bytes accessed | tf_op | source)
XLA Modules:
  0.0 261.3 jit_solution(10116042762897220651)
XLA Ops:
  0.7 254.2 %shard_map.305 = (bf16[4,256,1024]{2,1,0:T(8,128)(2,1)}, bf16[4,256,1024]{2,1,0:T(8,128)(2,1)}, f32[128,256]{1,0:T(8,128)}, f32[128,256]{1,0:T(8,128)}, f32[128,...) custom-call(s32[4]{0:T(128)} %lens.1, ...), custom_call_target="tpu_custom_call" | custom-call | tf_op jit(solution)/shard_map/pallas_call | solution.py:1082
  254.9 6.2 %shard_map.306 = (bf16[4,256,1024]{2,1,0:T(8,128)(2,1)}, f32[128,256]{1,0:T(8,128)}, f32[128,256]{1,0:T(8,128)}, f32[128,256]{1,0:T(8,128)}, f32[128,256]{1,0:T(...) custom-call(bf16[4,256,1024]{2,1,0:T(8,128)(2,1)} %get-tuple-element, ...), custom_call_target="tpu_custom_call" | custom-call | tf_op jit(solution)/shard_map/pallas_call | solution.py:1197

commit v6 on v5

--- a/solution.py
+++ b/solution.py
@@ -860,20 +860,20 @@
     attend_back(c)
     g_cross(0, 1)
     g_cross(0, 2)
+    g_cross(0, 3)
     for k in range(CHUNKS):
         ag_wait(dl1, 3, k, 0)
     attend_back(c_sib)
     for k in range(CHUNKS):
         ag_pass(dl1, 3, k)
-    g_cross(0, 3)
     g_cross(0, 0)
+    g_line(0)
     attend_back(c_y)
-    g_line(0)
+    g_cross(1, 1)
+    g_cross(1, 2)
     for k in range(CHUNKS):
         ag_wait(dl1, 3, k, 2)
     weight_grad(2, dl1, att)
-    g_cross(1, 1)
-    g_cross(1, 2)
     attend_back(c_ysib)
     g_relay(0)
     g_cross(1, 3)
@@ -901,7 +901,6 @@
     rs_sib(3, 1, in_back(c_sib))
     rs_own(3, in_back(c))
     weight_grad(3, x_tok, dqkv)
-    g_relay(1)
     sm[...] = jnp.sum(sums[...], 1)
 
     def sm_copy(stage, j, src, dst, dev):
@@ -927,6 +926,7 @@
         rows = pl.ds(k * chunk, chunk)
         pltpu.make_async_copy(gi_s.at[rows], gi_h.at[t, rows], line_r.at[k, 0]).start()
         hops(lambda ts, n, to: line_copy(k, gi_s, ts, n, to).start(), 0)
+    g_relay(1)
     g_line(2)
 
     def line_hop(k, h):

time: 262 us -> 259 us (0.989)
    pallas_call x1, Pallas kernels: 254 us -> 251 us  [shards(): pl.pallas_call(functools.partial(layer, dims), out_shape=(jax.ShapeDtypeS...]
where the time goes in v6:
time: 259 us
  Pallas kernels  258 us (100%)
    pallas_call x1, Pallas kernels, shards(): pl.pallas_call(functools.partial(layer, dims), out_shape=(jax.ShapeDtypeS...  251 us
    pallas_call x1, Pallas kernels, shards(): pl.pallas_call(functools.partial(hand_over, small_rows), grid=(nt,), out_...  6.2 us

profile of v6, /device:TPU:0, one launch (start us, length us, event | category | flops | bytes accessed | tf_op | source)
XLA Modules:
  0.0 258.5 jit_solution(3218792748272052315)
XLA Ops:
  0.7 251.5 %shard_map.305 = (bf16[4,256,1024]{2,1,0:T(8,128)(2,1)}, bf16[4,256,1024]{2,1,0:T(8,128)(2,1)}, f32[128,256]{1,0:T(8,128)}, f32[128,256]{1,0:T(8,128)}, f32[128,...) custom-call(s32[4]{0:T(128)} %lens.1, ...), custom_call_target="tpu_custom_call" | custom-call | tf_op jit(solution)/shard_map/pallas_call | solution.py:1082
  252.2 6.2 %shard_map.306 = (bf16[4,256,1024]{2,1,0:T(8,128)(2,1)}, f32[128,256]{1,0:T(8,128)}, f32[128,256]{1,0:T(8,128)}, f32[128,256]{1,0:T(8,128)}, f32[128,256]{1,0:T(...) custom-call(bf16[4,256,1024]{2,1,0:T(8,128)(2,1)} %get-tuple-element, ...), custom_call_target="tpu_custom_call" | custom-call | tf_op jit(solution)/shard_map/pallas_call | solution.py:1197

commit v7 on v6

--- a/solution.py
+++ b/solution.py
@@ -14,7 +14,7 @@
 BF16 = jnp.bfloat16
 TILE = 256
 ROWS = 16
-CHUNKS = 2
+CHUNKS = 4
 
 
 def dot(left, right):

time: 259 us -> 256 us (0.988)
  Pallas kernels: 258 us -> 254 us
    pallas_call x1, Pallas kernels: 251 us -> 248 us  [shards(): pl.pallas_call(functools.partial(layer, dims), out_shape=(jax.ShapeDtypeS...]
where the time goes in v7:
time: 256 us; the launch traced here: 255 us
  Pallas kernels  254 us (99%)
    pallas_call x1, Pallas kernels, shards(): pl.pallas_call(functools.partial(layer, dims), out_shape=(jax.ShapeDtypeS...  248 us
    pallas_call x1, Pallas kernels, shards(): pl.pallas_call(functools.partial(hand_over, small_rows), grid=(nt,), out_...  6.2 us

profile of v7, /device:TPU:0, one launch (start us, length us, event | category | flops | bytes accessed | tf_op | source)
XLA Modules:
  0.0 254.7 jit_solution(14638662884372892852)
XLA Ops:
  0.7 247.6 %shard_map.305 = (bf16[4,256,1024]{2,1,0:T(8,128)(2,1)}, bf16[4,256,1024]{2,1,0:T(8,128)(2,1)}, f32[128,256]{1,0:T(8,128)}, f32[128,256]{1,0:T(8,128)}, f32[128,...) custom-call(s32[4]{0:T(128)} %lens.1, ...), custom_call_target="tpu_custom_call" | custom-call | tf_op jit(solution)/shard_map/pallas_call | solution.py:1082
  248.3 6.2 %shard_map.306 = (bf16[4,256,1024]{2,1,0:T(8,128)(2,1)}, f32[128,256]{1,0:T(8,128)}, f32[128,256]{1,0:T(8,128)}, f32[128,256]{1,0:T(8,128)}, f32[128,256]{1,0:T(...) custom-call(bf16[4,256,1024]{2,1,0:T(8,128)(2,1)} %get-tuple-element, ...), custom_call_target="tpu_custom_call" | custom-call | tf_op jit(solution)/shard_map/pallas_call | solution.py:1197
